TPU v7x, 128 devices: a whole 4x4x4 slice. The times are simulated.
128 devices in a mesh: section: 8 (over y, core), seq: 16 (over z, x).
Axes of the slice: x: 4, y: 4, z: 4, core: 2. Of those that a mesh axis runs over, the one named last changes fastest.
Arguments:
- queries: bfloat16 [8, 2, 2048, 4096], P('section', None, 'seq'), may hold values from -20 to 20
- keys_values: bfloat16 [8, 2, 2048, 8, 256], P('section', None, 'seq'), may hold values from -20 to 20
- lengths: int32 [8, 2, 4], P('section'), may hold values from 1 to 1024, 2048 in all within a row
- order: int32 [8, 2], P('section'), may hold values from 0 to 1, each once within a row
Outputs:
- handoff: bfloat16 [8, 2, 2048, 4096], P('section', None, 'seq')
Inputs may be any that keep to these rules, and one draw needn't show every extreme that they name: Each row holds the lengths of 4 documents packed end to end, summing to 2048, the longest exactly 1024. `order`: each row is a permutation of the microbatch numbers.
All inputs are finite; a program needn't handle non-finite values.
Results may differ from a plain program's by a relative error of at most 0.0037.
Values may be sent and summed in bfloat16 or wider, within the bound.
No kernel may reach another device: no remote copies, remote signals or barrier semaphores. Data moves between devices by JAX's collectives and lax.ppermute only.
A program may use at most 64 MiB of HBM per device.

v0:
```python
import jax
import jax.numpy as jnp
from jax import lax
from jax.sharding import PartitionSpec as P

HD = 128
QH = 32
KVH = 8


def shortened(value):
    return jax.tree.map(lambda a: a.astype(jnp.bfloat16) if a.dtype == jnp.float32 else a, value)


def passed_along(block, axis, distance):
    devices = range(lax.axis_size(axis))
    route = [((i - distance) % len(devices), i) for i in devices]
    return lax.ppermute(block, axis, route)


def segment_ids(lengths_row, rows_all):
    ends = jnp.cumsum(lengths_row)
    position = jnp.arange(rows_all, dtype=jnp.int32)
    return jnp.sum((position[:, None] >= ends[None, :]).astype(jnp.int32), axis=1)


def attend(query_rows, pair_rows, lengths_row):
    rows_all = query_rows.shape[0]
    head_count = query_rows.shape[1] // HD
    pair_count = pair_rows.shape[1] // (2 * HD)
    share_count = head_count // pair_count
    scaling = HD ** (-0.5)
    segment = segment_ids(lengths_row, rows_all)
    position = jnp.arange(rows_all, dtype=jnp.int32)
    block_rows = min(512, rows_all)

    def one_block(block_index):
        row_start = block_index * block_rows
        query_block = lax.dynamic_slice_in_dim(query_rows, row_start, block_rows, 0)
        segment_query = lax.dynamic_slice_in_dim(segment, row_start, block_rows, 0)
        position_query = lax.dynamic_slice_in_dim(position, row_start, block_rows, 0)
        allowed = (segment_query[:, None] == segment[None, :]) & (
            position[None, :] <= position_query[:, None]
        )
        results = []
        for head_index in range(head_count):
            pair_head = head_index // share_count
            query_cols = query_block[:, head_index * HD : (head_index + 1) * HD]
            key_cols = pair_rows[:, pair_head * 2 * HD : pair_head * 2 * HD + HD]
            value_cols = pair_rows[:, pair_head * 2 * HD + HD : (pair_head + 1) * 2 * HD]
            scores = (
                lax.dot_general(
                    query_cols,
                    key_cols,
                    (((1,), (1,)), ((), ())),
                    preferred_element_type=jnp.float32,
                )
                * scaling
            )
            peaks = jnp.max(jnp.where(allowed, scores, -jnp.inf), axis=1, keepdims=True)
            weights = jnp.where(allowed, jnp.exp(scores - peaks), jnp.float32(0.0))
            totals = jnp.sum(weights, axis=1, keepdims=True)
            mixed = (
                jnp.dot(
                    weights.astype(jnp.bfloat16), value_cols, preferred_element_type=jnp.float32
                )
                / totals
            )
            results.append(mixed.astype(jnp.bfloat16))
        return jnp.concatenate(results, axis=1)

    blocks = lax.map(one_block, jnp.arange(rows_all // block_rows, dtype=jnp.int32))
    return blocks.reshape(rows_all, head_count * HD)


def reorder(stacked, order_row):
    picked_all = []
    for slot in range(stacked.shape[0]):
        picked = stacked[0]
        picked = jnp.where(order_row[slot] == 1, stacked[1], picked)
        picked_all.append(picked)
    return jnp.stack(picked_all, axis=0)


def local(queries, keys_values, lengths, order):
    n_seq = lax.axis_size("seq")
    micro = queries.shape[1]
    tok_rows = queries.shape[2]
    all_rows = tok_rows * n_seq
    per_device = QH // n_seq
    repeat_count = max(1, n_seq // KVH)
    kv_local = max(1, KVH // n_seq)
    query_split = queries.reshape(micro, tok_rows, n_seq, per_device * HD)
    wide = jnp.repeat(keys_values.reshape(micro, tok_rows, KVH, 2 * HD), repeat_count, axis=2)
    head_queries, head_pairs = (
        lax.all_to_all(query_split, "seq", split_axis=2, concat_axis=1, tiled=True),
        lax.all_to_all(wide, "seq", split_axis=2, concat_axis=1, tiled=True),
    )
    head_queries = head_queries.reshape(micro, all_rows, per_device * HD)
    head_pairs = head_pairs.reshape(micro, all_rows, kv_local * 2 * HD)
    contexts = jnp.stack(
        [
            attend(head_queries[index_mb], head_pairs[index_mb], lengths[0, index_mb])
            for index_mb in range(micro)
        ],
        axis=0,
    )
    contexts = contexts.reshape(micro, all_rows, 1, per_device * HD)
    back = lax.all_to_all(
        shortened(contexts), "seq", split_axis=1, concat_axis=2, tiled=True
    ).astype(contexts.dtype)
    result = passed_along(shortened(reorder(back, order[0])), "section", 1)
    return result.reshape(1, micro, tok_rows, QH * HD)


def solution(mesh):
    placed = (
        P("section", None, "seq", None),
        P("section", None, "seq", None, None),
        P("section", None, None),
        P("section", None),
    )
    return jax.shard_map(
        local,
        mesh=mesh,
        in_specs=placed,
        out_specs=P("section", None, "seq", None),
        check_vma=False,
    )
```

profile of v0, /device:TPU:0, one launch (start us, length us, event | category | flops | bytes accessed | tf_op | source)
XLA Modules:
  0.0 293.3 jit_solution(14216556808177884193)
XLA Ops:
  0.0 3.1 %copy.45 = bf16[1,2,128,4096]{2,3,1,0:T(8,128)(2,1)S(1)} copy(bf16[1,2,128,4096]{3,2,1,0:T(8,128)(2,1)} %param.8) | data formatting | bytes 4194304 | tf_op args[0]
  3.1 2.6 copy.46
  5.7 8.0 %all-to-all-start = ((bf16[2,128,16,256]{3,1,0,2:T(8,128)(2,1)}), bf16[2,128,16,256]{3,1,0,2:T(8,128)(2,1)S(1)}, u32[]{:S(2)}, u32[]{:S(2)}) async-start(bf16[2,128,16,256]{3,1,0,2:T(8,128)(2,1)} %copy.46), calls=%async_computation | async-start | bytes 4194304 | tf_op jit(solution)/shard_map/all_to_all | solution.py:96
  15.2 30.3 %all-to-all-done = bf16[2,128,16,256]{3,1,0,2:T(8,128)(2,1)S(1)} async-done(((bf16[2,128,16,256]{3,1,0,2:T(8,128)(2,1)}), bf16[2,128,16,256]{3,1,0,2:T(8,128)(2,1)S(1)}, u32[]{:S(2)}, u32[]{:S(2)}) %all-to-all-start) | async-done | bytes 2097184 | tf_op jit(solution)/shard_map/all_to_all | solution.py:96
  45.5 1.6 broadcast_in_dim.48
  47.1 4.4 %all-to-all-start.1 = ((bf16[2,128,16,256]{3,1,0,2:T(8,128)(2,1)}), bf16[2,128,16,256]{3,1,0,2:T(8,128)(2,1)}, u32[]{:S(2)}, u32[]{:S(2)}) async-start(bf16[2,128,16,256]{3,1,0,2:T(8,128)(2,1)} %bitcast.62), calls=%async_computation.1 | async-start | bytes 4194304 | tf_op jit(solution)/shard_map/all_to_all | solution.py:97
  53.6 27.9 %all-to-all-done.1 = bf16[2,128,16,256]{3,1,0,2:T(8,128)(2,1)} async-done(((bf16[2,128,16,256]{3,1,0,2:T(8,128)(2,1)}), bf16[2,128,16,256]{3,1,0,2:T(8,128)(2,1)}, u32[]{:S(2)}, u32[]{:S(2)}) %all-to-all-start.1) | async-done | bytes 2097184 | tf_op jit(solution)/shard_map/all_to_all | solution.py:97
  81.5 2.7 fusion.68
  84.3 59.1 %while.22 = (s32[]{:T(128)}, bf16[4,512,256]{2,1,0:T(8,128)(2,1)S(1)}, s32[4]{0:T(128)S(1)}, s32[2048]{0:T(1024)S(1)}, s32[2048]{0:T(1024)S(1)}, /*index=5*/bf16...) while((s32[]{:T(128)}, ...), condition=%wide.region_7.8_spmd.clone, body=%wide.region_2.7_spmd.clone.sunk | while | flops 1113323520 | bytes 46268652 | solution.py:72
  85.8 3.8 %select_reduce_fusion.6 = (f32[512]{0:T(512)S(1)}, f32[512,2048]{1,0:T(8,128)}) fusion(s32[512]{0:T(512)S(1)} %dynamic_slice.40, s32[2048]{0:T(1024)S(1)} %get-tuple-element.339, s32[2048]{0:T(1024)S(1)} %get-tuple-element.338, s32[512]{0:T(512)S(1)} %dynamic_slice.41, bf16[2048,256]{1,0:T(8,128)(2,1)S(1)} %get-tuple-element.341, ...), kind=kOutput, calls=%fused_computation.3.clone.1 | convolution fusion | flops 274726400 | bytes 4872196 | tf_op jit(solution)/shard_map/while/body/eval_jaxpr/dot_general | solution.py:52
  89.6 4.6 %fusion.91 = (f32[512]{0:T(512)S(1)}, f32[512]{0:T(512)S(1)}, f32[512,2048]{1,0:T(8,128)S(1)}) fusion(f32[512,2048]{1,0:T(8,128)} %get-tuple-element.258, f32[512]{0:T(512)S(1)} %get-tuple-element.259, s32[512]{0:T(512)S(1)} %dynamic_slice.40, s32[2048]{0:T(1024)S(1)} %get-tuple-element.339, s32[2048]{0:T(1024)S(1)} %get-tuple-element.338, ...), kind=kOutput, calls=%fused_computation.5.clone.1 | convolution fusion | flops 278920192 | bytes 9070600 | tf_op jit(solution)/shard_map/while/body/eval_jaxpr/dot_general | solution.py:52
  95.6 1.7 fusion.92
  100.6 3.8 %select_reduce_fusion.6 = (f32[512]{0:T(512)S(1)}, f32[512,2048]{1,0:T(8,128)}) fusion(s32[512]{0:T(512)S(1)} %dynamic_slice.40, s32[2048]{0:T(1024)S(1)} %get-tuple-element.339, s32[2048]{0:T(1024)S(1)} %get-tuple-element.338, s32[512]{0:T(512)S(1)} %dynamic_slice.41, bf16[2048,256]{1,0:T(8,128)(2,1)S(1)} %get-tuple-element.341, ...), kind=kOutput, calls=%fused_computation.3.clone.1 | convolution fusion | flops 274726400 | bytes 4872196 | tf_op jit(solution)/shard_map/while/body/eval_jaxpr/dot_general | solution.py:52
  104.4 4.6 %fusion.91 = (f32[512]{0:T(512)S(1)}, f32[512]{0:T(512)S(1)}, f32[512,2048]{1,0:T(8,128)S(1)}) fusion(f32[512,2048]{1,0:T(8,128)} %get-tuple-element.258, f32[512]{0:T(512)S(1)} %get-tuple-element.259, s32[512]{0:T(512)S(1)} %dynamic_slice.40, s32[2048]{0:T(1024)S(1)} %get-tuple-element.339, s32[2048]{0:T(1024)S(1)} %get-tuple-element.338, ...), kind=kOutput, calls=%fused_computation.5.clone.1 | convolution fusion | flops 278920192 | bytes 9070600 | tf_op jit(solution)/shard_map/while/body/eval_jaxpr/dot_general | solution.py:52
  110.4 1.7 fusion.92
  115.3 3.8 %select_reduce_fusion.6 = (f32[512]{0:T(512)S(1)}, f32[512,2048]{1,0:T(8,128)}) fusion(s32[512]{0:T(512)S(1)} %dynamic_slice.40, s32[2048]{0:T(1024)S(1)} %get-tuple-element.339, s32[2048]{0:T(1024)S(1)} %get-tuple-element.338, s32[512]{0:T(512)S(1)} %dynamic_slice.41, bf16[2048,256]{1,0:T(8,128)(2,1)S(1)} %get-tuple-element.341, ...), kind=kOutput, calls=%fused_computation.3.clone.1 | convolution fusion | flops 274726400 | bytes 4872196 | tf_op jit(solution)/shard_map/while/body/eval_jaxpr/dot_general | solution.py:52
  119.2 4.6 %fusion.91 = (f32[512]{0:T(512)S(1)}, f32[512]{0:T(512)S(1)}, f32[512,2048]{1,0:T(8,128)S(1)}) fusion(f32[512,2048]{1,0:T(8,128)} %get-tuple-element.258, f32[512]{0:T(512)S(1)} %get-tuple-element.259, s32[512]{0:T(512)S(1)} %dynamic_slice.40, s32[2048]{0:T(1024)S(1)} %get-tuple-element.339, s32[2048]{0:T(1024)S(1)} %get-tuple-element.338, ...), kind=kOutput, calls=%fused_computation.5.clone.1 | convolution fusion | flops 278920192 | bytes 9070600 | tf_op jit(solution)/shard_map/while/body/eval_jaxpr/dot_general | solution.py:52
  125.2 1.7 fusion.92
  130.1 3.8 %select_reduce_fusion.6 = (f32[512]{0:T(512)S(1)}, f32[512,2048]{1,0:T(8,128)}) fusion(s32[512]{0:T(512)S(1)} %dynamic_slice.40, s32[2048]{0:T(1024)S(1)} %get-tuple-element.339, s32[2048]{0:T(1024)S(1)} %get-tuple-element.338, s32[512]{0:T(512)S(1)} %dynamic_slice.41, bf16[2048,256]{1,0:T(8,128)(2,1)S(1)} %get-tuple-element.341, ...), kind=kOutput, calls=%fused_computation.3.clone.1 | convolution fusion | flops 274726400 | bytes 4872196 | tf_op jit(solution)/shard_map/while/body/eval_jaxpr/dot_general | solution.py:52
  133.9 4.6 %fusion.91 = (f32[512]{0:T(512)S(1)}, f32[512]{0:T(512)S(1)}, f32[512,2048]{1,0:T(8,128)S(1)}) fusion(f32[512,2048]{1,0:T(8,128)} %get-tuple-element.258, f32[512]{0:T(512)S(1)} %get-tuple-element.259, s32[512]{0:T(512)S(1)} %dynamic_slice.40, s32[2048]{0:T(1024)S(1)} %get-tuple-element.339, s32[2048]{0:T(1024)S(1)} %get-tuple-element.338, ...), kind=kOutput, calls=%fused_computation.5.clone.1 | convolution fusion | flops 278920192 | bytes 9070600 | tf_op jit(solution)/shard_map/while/body/eval_jaxpr/dot_general | solution.py:52
  140.0 1.7 fusion.92
  143.5 68.4 %while.23 = (s32[]{:T(128)}, bf16[4,512,256]{2,1,0:T(8,128)(2,1)S(1)}, s32[4]{0:T(128)S(1)}, s32[2048]{0:T(1024)S(1)}, s32[2048]{0:T(1024)S(1)}, /*index=5*/bf16...) while((s32[]{:T(128)}, ...), condition=%wide.region_15.16_spmd.clone, body=%wide.region_10.15_spmd.clone.sunk | while | flops 1113323520 | bytes 46268652 | solution.py:72
  145.1 4.0 %select_reduce_fusion.7 = (f32[512]{0:T(512)S(1)}, f32[512,2048]{1,0:T(8,128)}) fusion(s32[512]{0:T(512)S(1)} %dynamic_slice.43, s32[2048]{0:T(1024)S(1)} %get-tuple-element.303, s32[2048]{0:T(1024)S(1)} %get-tuple-element.302, s32[512]{0:T(512)S(1)} %dynamic_slice.44, bf16[2048,256]{1,0:T(8,128)(2,1)} %get-tuple-element.305, ...), kind=kOutput, calls=%fused_computation.33.clone.1 | convolution fusion | flops 274726400 | bytes 4872196 | tf_op jit(solution)/shard_map/while/body/eval_jaxpr/dot_general | solution.py:52
  149.1 4.7 %fusion.99 = (f32[512]{0:T(512)S(1)}, f32[512]{0:T(512)S(1)}, f32[512,2048]{1,0:T(8,128)S(1)}) fusion(f32[512,2048]{1,0:T(8,128)} %get-tuple-element.270, f32[512]{0:T(512)S(1)} %get-tuple-element.271, s32[512]{0:T(512)S(1)} %dynamic_slice.43, s32[2048]{0:T(1024)S(1)} %get-tuple-element.303, s32[2048]{0:T(1024)S(1)} %get-tuple-element.302, ...), kind=kOutput, calls=%fused_computation.35.clone.1 | convolution fusion | flops 278920192 | bytes 9070600 | tf_op jit(solution)/shard_map/while/body/eval_jaxpr/dot_general | solution.py:52
  153.8 2.5 fusion.102
  156.3 1.7 fusion.100
  158.0 2.5 fusion.101
  162.1 4.0 %select_reduce_fusion.7 = (f32[512]{0:T(512)S(1)}, f32[512,2048]{1,0:T(8,128)}) fusion(s32[512]{0:T(512)S(1)} %dynamic_slice.43, s32[2048]{0:T(1024)S(1)} %get-tuple-element.303, s32[2048]{0:T(1024)S(1)} %get-tuple-element.302, s32[512]{0:T(512)S(1)} %dynamic_slice.44, bf16[2048,256]{1,0:T(8,128)(2,1)} %get-tuple-element.305, ...), kind=kOutput, calls=%fused_computation.33.clone.1 | convolution fusion | flops 274726400 | bytes 4872196 | tf_op jit(solution)/shard_map/while/body/eval_jaxpr/dot_general | solution.py:52
  166.1 4.7 %fusion.99 = (f32[512]{0:T(512)S(1)}, f32[512]{0:T(512)S(1)}, f32[512,2048]{1,0:T(8,128)S(1)}) fusion(f32[512,2048]{1,0:T(8,128)} %get-tuple-element.270, f32[512]{0:T(512)S(1)} %get-tuple-element.271, s32[512]{0:T(512)S(1)} %dynamic_slice.43, s32[2048]{0:T(1024)S(1)} %get-tuple-element.303, s32[2048]{0:T(1024)S(1)} %get-tuple-element.302, ...), kind=kOutput, calls=%fused_computation.35.clone.1 | convolution fusion | flops 278920192 | bytes 9070600 | tf_op jit(solution)/shard_map/while/body/eval_jaxpr/dot_general | solution.py:52
  170.8 2.5 fusion.102
  173.3 1.7 fusion.100
  175.1 2.5 fusion.101
  179.2 4.0 %select_reduce_fusion.7 = (f32[512]{0:T(512)S(1)}, f32[512,2048]{1,0:T(8,128)}) fusion(s32[512]{0:T(512)S(1)} %dynamic_slice.43, s32[2048]{0:T(1024)S(1)} %get-tuple-element.303, s32[2048]{0:T(1024)S(1)} %get-tuple-element.302, s32[512]{0:T(512)S(1)} %dynamic_slice.44, bf16[2048,256]{1,0:T(8,128)(2,1)} %get-tuple-element.305, ...), kind=kOutput, calls=%fused_computation.33.clone.1 | convolution fusion | flops 274726400 | bytes 4872196 | tf_op jit(solution)/shard_map/while/body/eval_jaxpr/dot_general | solution.py:52
  183.2 4.7 %fusion.99 = (f32[512]{0:T(512)S(1)}, f32[512]{0:T(512)S(1)}, f32[512,2048]{1,0:T(8,128)S(1)}) fusion(f32[512,2048]{1,0:T(8,128)} %get-tuple-element.270, f32[512]{0:T(512)S(1)} %get-tuple-element.271, s32[512]{0:T(512)S(1)} %dynamic_slice.43, s32[2048]{0:T(1024)S(1)} %get-tuple-element.303, s32[2048]{0:T(1024)S(1)} %get-tuple-element.302, ...), kind=kOutput, calls=%fused_computation.35.clone.1 | convolution fusion | flops 278920192 | bytes 9070600 | tf_op jit(solution)/shard_map/while/body/eval_jaxpr/dot_general | solution.py:52
  187.9 2.5 fusion.102
  190.4 1.7 fusion.100
  192.1 2.5 fusion.101
  196.2 4.0 %select_reduce_fusion.7 = (f32[512]{0:T(512)S(1)}, f32[512,2048]{1,0:T(8,128)}) fusion(s32[512]{0:T(512)S(1)} %dynamic_slice.43, s32[2048]{0:T(1024)S(1)} %get-tuple-element.303, s32[2048]{0:T(1024)S(1)} %get-tuple-element.302, s32[512]{0:T(512)S(1)} %dynamic_slice.44, bf16[2048,256]{1,0:T(8,128)(2,1)} %get-tuple-element.305, ...), kind=kOutput, calls=%fused_computation.33.clone.1 | convolution fusion | flops 274726400 | bytes 4872196 | tf_op jit(solution)/shard_map/while/body/eval_jaxpr/dot_general | solution.py:52
  200.2 4.7 %fusion.99 = (f32[512]{0:T(512)S(1)}, f32[512]{0:T(512)S(1)}, f32[512,2048]{1,0:T(8,128)S(1)}) fusion(f32[512,2048]{1,0:T(8,128)} %get-tuple-element.270, f32[512]{0:T(512)S(1)} %get-tuple-element.271, s32[512]{0:T(512)S(1)} %dynamic_slice.43, s32[2048]{0:T(1024)S(1)} %get-tuple-element.303, s32[2048]{0:T(1024)S(1)} %get-tuple-element.302, ...), kind=kOutput, calls=%fused_computation.35.clone.1 | convolution fusion | flops 278920192 | bytes 9070600 | tf_op jit(solution)/shard_map/while/body/eval_jaxpr/dot_general | solution.py:52
  204.9 2.5 fusion.102
  207.4 1.7 fusion.100
  209.1 2.5 fusion.101
  212.1 14.0 %copy.50 = bf16[2,2048,1,256]{3,0,2,1:T(2,128)(2,1)} copy(bf16[2,2048,1,256]{3,1,0,2:T(8,128)(2,1)S(1)} %maximum_bitcast_fusion.2) | data formatting | bytes 4194304 | tf_op jit(solution)/shard_map/reshape | solution.py:108
  226.1 3.7 %all-to-all-start.2 = ((bf16[2,2048,1,256]{3,0,2,1:T(2,128)(2,1)}), bf16[2,2048,1,256]{3,0,2,1:T(2,128)(2,1)S(1)}, u32[]{:S(2)}, u32[]{:S(2)}) async-start(bf16[2,2048,1,256]{3,0,2,1:T(2,128)(2,1)} %copy.50), calls=%async_computation.2 | async-start | bytes 4194304 | tf_op jit(solution)/shard_map/all_to_all | solution.py:109
  231.8 28.2 %all-to-all-done.2 = bf16[2,2048,1,256]{3,0,2,1:T(2,128)(2,1)S(1)} async-done(((bf16[2,2048,1,256]{3,0,2,1:T(2,128)(2,1)}), bf16[2,2048,1,256]{3,0,2,1:T(2,128)(2,1)S(1)}, u32[]{:S(2)}, u32[]{:S(2)}) %all-to-all-start.2) | async-done | bytes 2097184 | tf_op jit(solution)/shard_map/all_to_all | solution.py:109
  260.7 26.8 %collective-permute-done = bf16[2,128,16,256]{3,1,2,0:T(8,128)(2,1)} collective-permute-done((bf16[2,128,16,256]{3,1,2,0:T(8,128)(2,1)S(1)}, bf16[2,128,16,256]{3,1,2,0:T(8,128)(2,1)}, u32[]{:S(2)}, u32[]{:S(2)}) %collective-permute-start) | collective-permute-done | bytes 2097184 | tf_op jit(solution)/shard_map/ppermute | solution.py:18
  287.5 3.0 %copy.55 = bf16[2,128,16,256]{1,3,2,0:T(8,128)(2,1)S(1)} copy(bf16[2,128,16,256]{3,1,2,0:T(8,128)(2,1)} %collective-permute-done) | data formatting | bytes 4194304 | tf_op jit(solution)/shard_map/ppermute | solution.py:18
  290.5 2.7 copy.56
  (96 shorter events, 24.7 us)
Async XLA Ops:
  5.7 39.8 %all-to-all-start = ((bf16[2,128,16,256]{3,1,0,2:T(8,128)(2,1)}), bf16[2,128,16,256]{3,1,0,2:T(8,128)(2,1)S(1)}, u32[]{:S(2)}, u32[]{:S(2)}) async-start(bf16[2,128,16,256]{3,1,0,2:T(8,128)(2,1)} %copy.46), calls=%async_computation | async-start | bytes 4194304 | tf_op jit(solution)/shard_map/all_to_all | solution.py:96
  15.2 36.3 %copy-start.1 = (s32[1,2,4]{2,1,0:T(2,128)S(1)}, s32[1,2,4]{2,1,0:T(2,128)}, u32[]{:S(2)}) copy-start(s32[1,2,4]{2,1,0:T(2,128)} %param.10) | copy-start | bytes 100
  47.1 34.4 %all-to-all-start.1 = ((bf16[2,128,16,256]{3,1,0,2:T(8,128)(2,1)}), bf16[2,128,16,256]{3,1,0,2:T(8,128)(2,1)}, u32[]{:S(2)}, u32[]{:S(2)}) async-start(bf16[2,128,16,256]{3,1,0,2:T(8,128)(2,1)} %bitcast.62), calls=%async_computation.1 | async-start | bytes 4194304 | tf_op jit(solution)/shard_map/all_to_all | solution.py:97
  89.6 4.6 %copy-start.2 = (f32[512,2048]{1,0:T(8,128)S(1)}, f32[512,2048]{1,0:T(8,128)}, u32[]{:S(2)}) copy-start(f32[512,2048]{1,0:T(8,128)} %get-tuple-element.258) | copy-start | bytes 12582916 | tf_op jit(solution)/shard_map/while
  104.4 4.6 %copy-start.2 = (f32[512,2048]{1,0:T(8,128)S(1)}, f32[512,2048]{1,0:T(8,128)}, u32[]{:S(2)}) copy-start(f32[512,2048]{1,0:T(8,128)} %get-tuple-element.258) | copy-start | bytes 12582916 | tf_op jit(solution)/shard_map/while
  119.2 4.6 %copy-start.2 = (f32[512,2048]{1,0:T(8,128)S(1)}, f32[512,2048]{1,0:T(8,128)}, u32[]{:S(2)}) copy-start(f32[512,2048]{1,0:T(8,128)} %get-tuple-element.258) | copy-start | bytes 12582916 | tf_op jit(solution)/shard_map/while
  133.9 4.6 %copy-start.2 = (f32[512,2048]{1,0:T(8,128)S(1)}, f32[512,2048]{1,0:T(8,128)}, u32[]{:S(2)}) copy-start(f32[512,2048]{1,0:T(8,128)} %get-tuple-element.258) | copy-start | bytes 12582916 | tf_op jit(solution)/shard_map/while
  149.1 4.7 %copy-start.3 = (f32[512,2048]{1,0:T(8,128)S(1)}, f32[512,2048]{1,0:T(8,128)}, u32[]{:S(2)}) copy-start(f32[512,2048]{1,0:T(8,128)} %get-tuple-element.270) | copy-start | bytes 12582916 | tf_op jit(solution)/shard_map/while
  166.1 4.7 %copy-start.3 = (f32[512,2048]{1,0:T(8,128)S(1)}, f32[512,2048]{1,0:T(8,128)}, u32[]{:S(2)}) copy-start(f32[512,2048]{1,0:T(8,128)} %get-tuple-element.270) | copy-start | bytes 12582916 | tf_op jit(solution)/shard_map/while
  183.2 4.7 %copy-start.3 = (f32[512,2048]{1,0:T(8,128)S(1)}, f32[512,2048]{1,0:T(8,128)}, u32[]{:S(2)}) copy-start(f32[512,2048]{1,0:T(8,128)} %get-tuple-element.270) | copy-start | bytes 12582916 | tf_op jit(solution)/shard_map/while
  200.2 4.7 %copy-start.3 = (f32[512,2048]{1,0:T(8,128)S(1)}, f32[512,2048]{1,0:T(8,128)}, u32[]{:S(2)}) copy-start(f32[512,2048]{1,0:T(8,128)} %get-tuple-element.270) | copy-start | bytes 12582916 | tf_op jit(solution)/shard_map/while
  212.0 17.7 %copy-start = (s32[1,2]{1,0:T(1,128)S(1)}, s32[1,2]{1,0:T(1,128)}, u32[]{:S(2)}) copy-start(s32[1,2]{1,0:T(1,128)} %param.11) | copy-start | bytes 28
  226.1 33.9 %all-to-all-start.2 = ((bf16[2,2048,1,256]{3,0,2,1:T(2,128)(2,1)}), bf16[2,2048,1,256]{3,0,2,1:T(2,128)(2,1)S(1)}, u32[]{:S(2)}, u32[]{:S(2)}) async-start(bf16[2,2048,1,256]{3,0,2,1:T(2,128)(2,1)} %copy.50), calls=%async_computation.2 | async-start | bytes 4194304 | tf_op jit(solution)/shard_map/all_to_all | solution.py:109
  260.7 26.8 %collective-permute-start = (bf16[2,128,16,256]{3,1,2,0:T(8,128)(2,1)S(1)}, bf16[2,128,16,256]{3,1,2,0:T(8,128)(2,1)}, u32[]{:S(2)}, u32[]{:S(2)}) collective-permute-start(bf16[2,128,16,256]{3,1,2,0:T(8,128)(2,1)S(1)} %pad_maximum_fusion), channel_id=1, source_target_pairs={{112,0},{0,16},{16,32},{32,48},{48,64},{64,80},{80,96},{96,112},{1... | collective-permute-start | bytes 6291464 | tf_op jit(solution)/shard_map/ppermute | solution.py:18
where the time goes:
time: 294 us; the launch traced here: 293 us
  waiting for transfers between devices  113 us (38%)
  matrix products  99.9 us (34%)
  local copies, waits for them, and re-layouts  41.4 us (14%)
  starting transfers between devices  16.2 us (6%)
  other arithmetic  15.1 us (5%)
  loops' own time  6.04 us (2%)
    dot_general x16, matrix products, one_block(): lax.dot_general(query_cols, key_cols, (((1,), (1,)), ((), ())), preferred...  68.2 us
    dot_general x16, matrix products, one_block(): jnp.dot(weights.astype(jnp.bfloat16), value_cols, preferred_element_type=...  31.6 us
    all_to_all x1, waiting for transfers between devices, local(): lax.all_to_all(query_split, 'seq', split_axis=2, concat_axis=1, tiled=True)  30.3 us
    all_to_all x1, waiting for transfers between devices, local(): lax.all_to_all(shortened(contexts), 'seq', split_axis=1, concat_axis=2, t...  28.2 us
    all_to_all x1, waiting for transfers between devices, local(): lax.all_to_all(wide, 'seq', split_axis=2, concat_axis=1, tiled=True)  27.9 us
    ppermute x1, waiting for transfers between devices, passed_along(): return lax.ppermute(block, axis, route)  26.8 us
    reshape x1, local copies, waits for them, and re-layouts, local(): contexts = contexts.reshape(micro, all_rows, 1, per_device * HD)  14 us
    reduce_sum x8, other arithmetic, one_block(): totals = jnp.sum(weights, axis=1, keepdims=True)  13.8 us
  transfers between devices with their start and end apart: 4, of which 4 were waited for; matrix products, arithmetic and copies ran while one was open for 1% of the time, Pallas kernels for 0%

commit v1 on v0

v1 whole, which is shorter than its diff:
```python
import functools

import jax
import jax.numpy as jnp
from jax import lax
from jax.experimental import pallas as pl
from jax.experimental.pallas import tpu as pltpu
from jax.sharding import PartitionSpec as P

HD = 128
QH = 32
KVH = 8
MB = 2
SHARE = QH // KVH
BLOCK = 128
EXPONENT = 1.4426950408889634 * HD ** (-0.5)
WINDOWS = (2, 4, 6, 8, 9)


def pack_kernel(q_ref, kv_ref, o_ref):
    wide = SHARE * HD
    for g in range(KVH):
        o_ref[g, :, 0:wide] = q_ref[0, 0, :, g * wide : (g + 1) * wide]
        o_ref[g, :, wide : wide + 2 * HD] = kv_ref[0, 0, :, g, :]


def pack(queries, keys_values):
    rows = queries.shape[2]
    wide = SHARE * HD + 2 * HD
    return pl.pallas_call(
        pack_kernel,
        out_shape=jax.ShapeDtypeStruct((MB * KVH, rows, wide), jnp.bfloat16),
        grid=(MB,),
        in_specs=[
            pl.BlockSpec((1, 1, rows, QH * HD), lambda m: (0, m, 0, 0)),
            pl.BlockSpec((1, 1, rows, KVH, 2 * HD), lambda m: (0, m, 0, 0, 0)),
        ],
        out_specs=pl.BlockSpec((KVH, rows, wide), lambda m: (m, 0, 0)),
        name="pack",
    )(queries, keys_values)


def attend_kernel(len_ref, q_ref, kv_ref, o_ref, ve_ref):
    i = pl.program_id(0)
    m = lax.axis_index("seq") // KVH

    @pl.when(i == 0)
    def _():
        ve_ref[:, 0:HD] = kv_ref[:, HD : 2 * HD]
        ve_ref[:, HD : 2 * HD] = jnp.ones((ve_ref.shape[0], HD), jnp.bfloat16)

    end0 = len_ref[0, m, 0]
    end1 = end0 + len_ref[0, m, 1]
    end2 = end1 + len_ref[0, m, 2]

    def start_of(t):
        late = jnp.where(t < end1, end0, jnp.where(t < end2, end1, end2))
        return jnp.where(t < end0, 0, late)

    first = i * BLOCK
    need = i + 1 - start_of(first) // BLOCK
    token = first + lax.broadcasted_iota(jnp.int32, (BLOCK, HD), 0)
    begin = start_of(token)
    lane = lax.broadcasted_iota(jnp.int32, (BLOCK, HD), 1)
    pair = 2

    def window(n):
        low = pl.multiple_of(jnp.maximum(i + 1 - n, 0) * BLOCK, BLOCK)
        keys = kv_ref[pl.ds(low, n * BLOCK), 0:HD]
        values = ve_ref[pl.ds(low, n * BLOCK), :]
        for h0 in range(0, SHARE, pair):
            heads = range(h0, h0 + pair)
            q = jnp.concatenate([q_ref[:, h * HD : (h + 1) * HD] for h in heads], axis=0)
            scores = lax.dot_general(
                q, keys, (((1,), (1,)), ((), ())), preferred_element_type=jnp.float32
            )
            tiles = []
            for j in range(n):
                key = low + j * BLOCK + lane
                allowed = key >= begin
                if j >= n - 2:
                    allowed = allowed & (key <= token)
                allowed = jnp.concatenate([allowed] * pair, axis=0)
                tiles.append(jnp.where(allowed, scores[:, j * BLOCK : (j + 1) * BLOCK], -jnp.inf))
            top = functools.reduce(jnp.maximum, tiles)
            peak = jnp.max(top, axis=1, keepdims=True) * EXPONENT
            weights = [jnp.exp2(t * EXPONENT - peak).astype(jnp.bfloat16) for t in tiles]
            mixed = jnp.dot(
                jnp.concatenate(weights, axis=1), values, preferred_element_type=jnp.float32
            )
            out = (mixed[:, 0:HD] / mixed[:, HD : 2 * HD]).astype(jnp.bfloat16)
            for k, h in enumerate(heads):
                o_ref[:, h * HD : (h + 1) * HD] = out[k * BLOCK : (k + 1) * BLOCK, :]

    below = 0
    for n in WINDOWS:
        pl.when((need > below) & (need <= n))(functools.partial(window, n))
        below = n


def attend(packed, lengths):
    tokens = packed.shape[0]
    wide = SHARE * HD
    return pl.pallas_call(
        attend_kernel,
        out_shape=jax.ShapeDtypeStruct((tokens, wide), jnp.bfloat16),
        grid_spec=pltpu.PrefetchScalarGridSpec(
            num_scalar_prefetch=1,
            grid=(tokens // BLOCK,),
            in_specs=[
                pl.BlockSpec((BLOCK, wide), lambda i, n: (i, 0)),
                pl.BlockSpec(
                    (tokens, 2 * HD), lambda i, n: (0, 2), pipeline_mode=pl.Buffered(1)
                ),
            ],
            out_specs=pl.BlockSpec((BLOCK, wide), lambda i, n: (i, 0)),
            scratch_shapes=[pltpu.VMEM((tokens, 2 * HD), jnp.bfloat16)],
        ),
        name="attend",
    )(lengths, packed, packed)


def unpack_kernel(order_ref, r_ref, o_ref):
    wide = SHARE * HD
    for g in range(KVH):
        o_ref[0, 0, :, g * wide : (g + 1) * wide] = r_ref[g]


def unpack(blocks, order):
    rows = blocks.shape[1]
    wide = SHARE * HD
    return pl.pallas_call(
        unpack_kernel,
        out_shape=jax.ShapeDtypeStruct((1, MB, rows, QH * HD), jnp.bfloat16),
        grid_spec=pltpu.PrefetchScalarGridSpec(
            num_scalar_prefetch=1,
            grid=(MB,),
            in_specs=[pl.BlockSpec((KVH, rows, wide), lambda j, o: (o[0, j], 0, 0))],
            out_specs=pl.BlockSpec((1, 1, rows, QH * HD), lambda j, o: (0, j, 0, 0)),
        ),
        name="unpack",
    )(order, blocks)


def exchange(blocks):
    return lax.all_to_all(blocks, "seq", split_axis=0, concat_axis=0, tiled=True)


def local(queries, keys_values, lengths, order):
    n_seq = MB * KVH
    rows = queries.shape[2]
    packed = exchange(pack(queries, keys_values))
    context = attend(packed.reshape(n_seq * rows, -1), lengths)
    back = exchange(context.reshape(n_seq, rows, SHARE * HD))
    sections = lax.axis_size("section")
    route = [(i, (i + 1) % sections) for i in range(sections)]
    return lax.ppermute(unpack(back, order), "section", route)


def solution(mesh):
    placed = (
        P("section", None, "seq", None),
        P("section", None, "seq", None, None),
        P("section", None, None),
        P("section", None),
    )
    return jax.shard_map(
        local,
        mesh=mesh,
        in_specs=placed,
        out_specs=P("section", None, "seq", None),
        check_vma=False,
    )
```

time: 294 us -> 134 us (0.46)
  matrix products: 99.9 us -> 0 us
  waiting for transfers between devices: 113 us -> 26.9 us
  blocking collectives: 0 us -> 79.7 us
  local copies, waits for them, and re-layouts: 41.4 us -> 1.32 us
  Pallas kernels: 0 us -> 24.7 us
  starting transfers between devices: 16.2 us -> 0.01 us
  other arithmetic: 15.1 us -> 0 us
  loops' own time: 6.04 us -> 0 us
    dot_general x32 -> x0, matrix products: 99.9 us -> none  [the longest x16 68.2 us: one_block(): lax.dot_general(query_cols, key_cols, (((1,), (1,)), ((), ())), preferred...]
    all_to_all x3 -> x0, waiting for transfers between devices: 86.4 us -> none  [the longest x1 30.3 us: local(): lax.all_to_all(query_split, 'seq', split_axis=2, concat_axis=1, tiled=True)]
    all_to_all x0 -> x2, blocking collectives: none -> 79.7 us  [exchange(): lax.all_to_all(blocks, 'seq', split_axis=0, concat_axis=0, tiled=True)]
    pallas_call x0 -> x3, Pallas kernels: none -> 24.7 us  [the longest x1 17.4 us: attend(): pl.pallas_call(attend_kernel, out_shape=jax.ShapeDtypeStruct((tokens, wid...]
    reshape x4 -> x0, local copies, waits for them, and re-layouts: 20.8 us -> none  [the longest x1 14 us: local(): contexts = contexts.reshape(micro, all_rows, 1, per_device * HD)]
    all_to_all x3 -> x0, starting transfers between devices: 16.1 us -> none  [the longest x1 7.99 us: local(): lax.all_to_all(query_split, 'seq', split_axis=2, concat_axis=1, tiled=True)]
    reduce_sum x10 -> x0, other arithmetic: 14 us -> none  [the longest x8 13.8 us: one_block(): totals = jnp.sum(weights, axis=1, keepdims=True)]
    dynamic_slice x24 -> x0, local copies, waits for them, and re-layouts: 6.34 us -> none  [the longest x8 5.12 us: attend(): lax.map(one_block, jnp.arange(rows_all // block_rows, dtype=jnp.int32))]
  transfers between devices with their start and end apart: 4 -> 1, of which waited for: 4 -> 1; matrix products, arithmetic and copies ran while one was open for 1% -> 0% of each run, Pallas kernels for 0% -> 0%
where the time goes in v1:
time: 134 us; the launch traced here: 133 us
  blocking collectives  79.7 us (59%)
  waiting for transfers between devices  26.9 us (20%)
  Pallas kernels  24.7 us (18%)
    all_to_all x2, blocking collectives, exchange(): lax.all_to_all(blocks, 'seq', split_axis=0, concat_axis=0, tiled=True)  79.7 us
    ppermute x1, waiting for transfers between devices, local(): return lax.ppermute(unpack(back, order), 'section', route)  26.9 us
    pallas_call x1, Pallas kernels, attend(): pl.pallas_call(attend_kernel, out_shape=jax.ShapeDtypeStruct((tokens, wid...  17.4 us
    pallas_call x1, Pallas kernels, pack(): pl.pallas_call(pack_kernel, out_shape=jax.ShapeDtypeStruct((MB * KVH, row...  4.07 us
    pallas_call x1, Pallas kernels, unpack(): pl.pallas_call(unpack_kernel, out_shape=jax.ShapeDtypeStruct((1, MB, rows...  3.29 us
  transfers between devices with their start and end apart: 1, of which 1 were waited for; matrix products, arithmetic and copies ran while one was open for 0% of the time, Pallas kernels for 0%

profile of v1, /device:TPU:0, one launch (start us, length us, event | category | flops | bytes accessed | tf_op | source)
XLA Modules:
  0.0 132.7 jit_solution(5985535308180457120)
XLA Ops:
  0.0 4.1 %pack.1 = bf16[16,128,768]{2,1,0:T(8,128)(2,1)} custom-call(bf16[1,2,128,4096]{3,2,1,0:T(8,128)(2,1)} %q_ref.1, bf16[1,2,128,8,256]{4,3,2,1,0:T(8,128)(2,1)} %kv_ref.1), custom_call_target="tpu_custom_call" | custom-call | tf_op jit(solution)/shard_map/pack/pallas_call | solution.py:30
  4.1 47.7 %all_to_all.10 = bf16[16,128,768]{2,1,0:T(8,128)(2,1)} all-to-all(bf16[16,128,768]{2,1,0:T(8,128)(2,1)} %pack.1), channel_id=1, replica_groups=mesh['section'=8,'seq'=16] {'seq'}, dimensions={0} | all-to-all | bytes 6291456 | tf_op jit(solution)/shard_map/all_to_all | solution.py:146
  51.8 17.4 %attend.1 = bf16[2048,512]{1,0:T(8,128)(2,1)} custom-call(s32[1,2,4]{2,1,0:T(2,128)} %len_ref.1, bf16[2048,768]{1,0:T(8,128)(2,1)} %bitcast.2, bf16[2048,768]{1,0:T(8,128)(2,1)} %bitcast.3), custom_call_target="tpu_custom_call" | custom-call | tf_op jit(solution)/shard_map/attend/pallas_call | solution.py:104
  69.2 32.0 %all_to_all.11.r_ref = bf16[16,128,512]{2,1,0:T(8,128)(2,1)} all-to-all(bf16[16,128,512]{2,1,0:T(8,128)(2,1)} %bitcast.4), channel_id=1, replica_groups=mesh['section'=8,'seq'=16] {'seq'}, dimensions={0} | all-to-all | bytes 4194304 | tf_op jit(solution)/shard_map/all_to_all | solution.py:146
  101.2 3.3 %unpack.1 = bf16[1,2,128,4096]{3,2,1,0:T(8,128)(2,1)} custom-call(s32[1,2]{1,0:T(1,128)} %order_ref.1, bf16[16,128,512]{2,1,0:T(8,128)(2,1)} %all_to_all.11.r_ref), custom_call_target="tpu_custom_call" | custom-call | tf_op jit(solution)/shard_map/unpack/pallas_call | solution.py:132
  104.5 0.0 collective-permute-start
  104.5 26.9 %collective-permute-done = bf16[1,2,128,4096]{3,2,1,0:T(8,128)(2,1)S(1)} collective-permute-done((bf16[1,2,128,4096]{3,2,1,0:T(8,128)(2,1)}, bf16[1,2,128,4096]{3,2,1,0:T(8,128)(2,1)S(1)}, u32[]{:S(2)}, u32[]{:S(2)}) %collective-permute-start) | collective-permute-done | bytes 2097184 | tf_op jit(solution)/shard_map/ppermute | solution.py:157
  131.3 1.3 copy.6
Async XLA Ops:
  104.5 26.9 %collective-permute-start = (bf16[1,2,128,4096]{3,2,1,0:T(8,128)(2,1)}, bf16[1,2,128,4096]{3,2,1,0:T(8,128)(2,1)S(1)}, u32[]{:S(2)}, u32[]{:S(2)}) collective-permute-start(bf16[1,2,128,4096]{3,2,1,0:T(8,128)(2,1)} %unpack.1), channel_id=1, source_target_pairs={{0,16},{16,32},{32,48},{48,64},{64,80},{80,96},{96,112},{112,0},{1... | collective-permute-start | bytes 6291464 | tf_op jit(solution)/shard_map/ppermute | solution.py:157

commit v2 on v1

v2 whole, which is shorter than its diff:
```python
import functools

import jax
import jax.numpy as jnp
from jax import lax
from jax.experimental import pallas as pl
from jax.experimental.pallas import tpu as pltpu
from jax.sharding import PartitionSpec as P

HD = 128
QH = 32
KVH = 8
MB = 2
SHARE = QH // KVH
ROWS = 256
TILE = 128
NEAR = SHARE // 2
EXPONENT = 1.4426950408889634 * HD ** (-0.5)
WINDOWS = 5


def pack_kernel(order_ref, q_ref, kv_ref, o_ref):
    wide = SHARE * HD
    for g in range(KVH):
        o_ref[g, :, 0:wide] = q_ref[0, 0, :, g * wide : (g + 1) * wide]
        o_ref[g, :, wide : wide + 2 * HD] = kv_ref[0, 0, :, g, :]


def pack(queries, keys_values, order):
    rows = queries.shape[2]
    wide = SHARE * HD + 2 * HD
    return pl.pallas_call(
        pack_kernel,
        out_shape=jax.ShapeDtypeStruct((MB * KVH, rows, wide), jnp.bfloat16),
        grid_spec=pltpu.PrefetchScalarGridSpec(
            num_scalar_prefetch=1,
            grid=(MB,),
            in_specs=[
                pl.BlockSpec((1, 1, rows, QH * HD), lambda j, o: (0, o[0, j], 0, 0)),
                pl.BlockSpec((1, 1, rows, KVH, 2 * HD), lambda j, o: (0, o[0, j], 0, 0, 0)),
            ],
            out_specs=pl.BlockSpec((KVH, rows, wide), lambda j, o: (j, 0, 0)),
        ),
        name="pack",
    )(order, queries, keys_values)


def attend_kernel(len_ref, order_ref, q_ref, kv_ref, near_ref, far_ref, ve_ref, s_ref, m_ref):
    i = pl.program_id(0)
    m = order_ref[0, lax.axis_index("seq") // KVH]

    @pl.when(i == 0)
    def _():
        ve_ref[:, 0:HD] = kv_ref[:, HD : 2 * HD]
        ve_ref[:, HD : 2 * HD] = jnp.ones((ve_ref.shape[0], HD), jnp.bfloat16)

    end0 = len_ref[0, m, 0]
    end1 = end0 + len_ref[0, m, 1]
    end2 = end1 + len_ref[0, m, 2]

    def start_of(t):
        late = jnp.where(t < end1, end0, jnp.where(t < end2, end1, end2))
        return jnp.where(t < end0, 0, late)

    need = i + 1 - start_of(i * ROWS) // ROWS
    token = i * ROWS + lax.broadcasted_iota(jnp.int32, (ROWS, TILE), 0)
    begin = start_of(token)
    lane = lax.broadcasted_iota(jnp.int32, (ROWS, TILE), 1)
    pair = 2
    last = ROWS // TILE

    def window(n):
        low = pl.multiple_of((i + 1 - n) * ROWS, ROWS)
        tiles = n * ROWS // TILE

        def score(g):
            heads = range(g * pair, (g + 1) * pair)
            q = jnp.concatenate([q_ref[:, h * HD : (h + 1) * HD] for h in heads], axis=0)
            scores = lax.dot_general(
                q,
                kv_ref[pl.ds(low, n * ROWS), 0:HD],
                (((1,), (1,)), ((), ())),
                preferred_element_type=jnp.float32,
            )
            top = None
            for j in range(tiles):
                key = low + j * TILE + lane
                allowed = key >= begin
                if j >= tiles - last:
                    allowed = allowed & (key <= token)
                allowed = jnp.concatenate([allowed] * pair, axis=0)
                tile = jnp.where(allowed, scores[:, j * TILE : (j + 1) * TILE], -jnp.inf)
                s_ref[g, :, j * TILE : (j + 1) * TILE] = tile
                top = tile if top is None else jnp.maximum(top, tile)
            peak = jnp.max(top, axis=1, keepdims=True)
            m_ref[g] = jnp.broadcast_to(peak, (pair * ROWS, TILE))

        def mix(g, o_ref):
            peak = m_ref[g]
            weights = [
                jnp.exp2((s_ref[g, :, j * TILE : (j + 1) * TILE] - peak) * EXPONENT).astype(
                    jnp.bfloat16
                )
                for j in range(tiles)
            ]
            mixed = jnp.dot(
                jnp.concatenate(weights, axis=1),
                ve_ref[pl.ds(low, n * ROWS), :],
                preferred_element_type=jnp.float32,
            )
            out = (mixed[:, 0:HD] / mixed[:, HD : 2 * HD]).astype(jnp.bfloat16)
            for h in range(pair):
                o_ref[:, h * HD : (h + 1) * HD] = out[h * ROWS : (h + 1) * ROWS, :]

        score(0)
        score(1)
        mix(0, near_ref)
        mix(1, far_ref)

    for n in range(1, WINDOWS + 1):
        pl.when(need == n)(functools.partial(window, n))


def attend(packed, lengths, order):
    tokens = packed.shape[0]
    wide = SHARE * HD
    half = NEAR * HD
    return pl.pallas_call(
        attend_kernel,
        out_shape=[jax.ShapeDtypeStruct((tokens, half), jnp.bfloat16)] * 2,
        grid_spec=pltpu.PrefetchScalarGridSpec(
            num_scalar_prefetch=2,
            grid=(tokens // ROWS,),
            in_specs=[
                pl.BlockSpec((ROWS, wide), lambda i, n, o: (i, 0)),
                pl.BlockSpec(
                    (tokens, 2 * HD), lambda i, n, o: (0, 2), pipeline_mode=pl.Buffered(1)
                ),
            ],
            out_specs=[pl.BlockSpec((ROWS, half), lambda i, n, o: (i, 0))] * 2,
            scratch_shapes=[
                pltpu.VMEM((tokens, 2 * HD), jnp.bfloat16),
                pltpu.VMEM((2, NEAR * ROWS, WINDOWS * ROWS), jnp.float32),
                pltpu.VMEM((2, NEAR * ROWS, TILE), jnp.float32),
            ],
        ),
        name="attend",
    )(lengths, order, packed, packed)


def unpack_kernel(near_ref, far_ref, o_ref, sems):
    copies = []
    for k in range(MB * KVH):
        for p, ref in enumerate((near_ref, far_ref)):
            part = ref.shape[2]
            col = (k % KVH) * SHARE * HD + p * part
            copies.append(
                pltpu.make_async_copy(
                    ref.at[k], o_ref.at[0, k // KVH, :, pl.ds(col, part)], sems.at[p, k]
                )
            )
    for copy in copies:
        copy.start()
    for copy in copies:
        copy.wait()


def unpack(near, far):
    rows = near.shape[1]
    return pl.pallas_call(
        unpack_kernel,
        out_shape=jax.ShapeDtypeStruct((1, MB, rows, QH * HD), jnp.bfloat16),
        in_specs=[pl.BlockSpec(memory_space=pltpu.VMEM)] * 2,
        out_specs=pl.BlockSpec(memory_space=pl.ANY),
        scratch_shapes=[pltpu.SemaphoreType.DMA((2, MB * KVH))],
        compiler_params=pltpu.CompilerParams(vmem_limit_bytes=8 << 20),
        name="unpack",
    )(near, far)


def exchange(blocks):
    return lax.all_to_all(blocks, "seq", split_axis=0, concat_axis=0, tiled=True)


def handed_on(block):
    sections = lax.axis_size("section")
    return lax.ppermute(block, "section", [(i, (i + 1) % sections) for i in range(sections)])


def handed_on(block):
    sections = lax.axis_size("section")
    return lax.ppermute(block, "section", [(i, (i + 1) % sections) for i in range(sections)])


def local(queries, keys_values, lengths, order):
    n_seq = MB * KVH
    rows = queries.shape[2]
    packed = exchange(pack(queries, keys_values, order)).reshape(n_seq * rows, -1)
    near, far = attend(packed, lengths, order)
    far = handed_on(far)
    near = handed_on(exchange(near.reshape(n_seq, rows, -1)))
    far = exchange(far.reshape(n_seq, rows, -1))
    return unpack(near, far)


def solution(mesh):
    placed = (
        P("section", None, "seq", None),
        P("section", None, "seq", None, None),
        P("section", None, None),
        P("section", None),
    )
    return jax.shard_map(
        local,
        mesh=mesh,
        in_specs=placed,
        out_specs=P("section", None, "seq", None),
        check_vma=False,
    )
```

time: 134 us -> 111 us (0.83)
  blocking collectives: 79.7 us -> 47.7 us
  starting transfers between devices: 0.01 us -> 10.3 us
  Pallas kernels: 24.7 us -> 18.5 us
  waiting for transfers between devices: 26.9 us -> 32.6 us
    all_to_all x2 -> x1, blocking collectives: 79.7 us -> 47.7 us  [exchange(): lax.all_to_all(blocks, 'seq', split_axis=0, concat_axis=0, tiled=True)]
    all_to_all x0 -> x2, waiting for transfers between devices: none -> 24.8 us  [exchange(): lax.all_to_all(blocks, 'seq', split_axis=0, concat_axis=0, tiled=True)]
    ppermute x1 -> x2, waiting for transfers between devices: 26.9 us -> 7.88 us  [handed_on(): lax.ppermute(block, 'section', [(i, (i + 1) % sections) for i in range(se...]
    all_to_all x0 -> x2, starting transfers between devices: none -> 10.3 us  [exchange(): lax.all_to_all(blocks, 'seq', split_axis=0, concat_axis=0, tiled=True)]
    pallas_call x1, Pallas kernels: 17.4 us -> 12.2 us  [attend(): pl.pallas_call(attend_kernel, out_shape=[jax.ShapeDtypeStruct((tokens, ha...]
    pallas_call x1, Pallas kernels: 3.29 us -> 1.57 us  [unpack(): pl.pallas_call(unpack_kernel, out_shape=jax.ShapeDtypeStruct((1, MB, rows...]
  transfers between devices with their start and end apart: 1 -> 4, of which waited for: 1 -> 3; matrix products, arithmetic and copies ran while one was open for 0% -> 0% of each run, Pallas kernels for 0% -> 0%
where the time goes in v2:
time: 111 us; the launch traced here: 110 us
  blocking collectives  47.7 us (43%)
  waiting for transfers between devices  32.6 us (29%)
  Pallas kernels  18.5 us (17%)
  starting transfers between devices  10.3 us (9%)
    all_to_all x1, blocking collectives, exchange(): lax.all_to_all(blocks, 'seq', split_axis=0, concat_axis=0, tiled=True)  47.7 us
    all_to_all x2, waiting for transfers between devices, exchange(): lax.all_to_all(blocks, 'seq', split_axis=0, concat_axis=0, tiled=True)  24.8 us
    pallas_call x1, Pallas kernels, attend(): pl.pallas_call(attend_kernel, out_shape=[jax.ShapeDtypeStruct((tokens, ha...  12.2 us
    all_to_all x2, starting transfers between devices, exchange(): lax.all_to_all(blocks, 'seq', split_axis=0, concat_axis=0, tiled=True)  10.3 us
    ppermute x2, waiting for transfers between devices, handed_on(): lax.ppermute(block, 'section', [(i, (i + 1) % sections) for i in range(se...  7.88 us
    pallas_call x1, Pallas kernels, pack(): pl.pallas_call(pack_kernel, out_shape=jax.ShapeDtypeStruct((MB * KVH, row...  4.78 us
  transfers between devices with their start and end apart: 4, of which 3 were waited for; matrix products, arithmetic and copies ran while one was open for 0% of the time, Pallas kernels for 0%

profile of v2, /device:TPU:0, one launch (start us, length us, event | category | flops | bytes accessed | tf_op | source)
XLA Modules:
  0.0 110.2 jit_solution(3825970952726905307)
XLA Ops:
  0.0 4.8 %pack.1 = bf16[16,128,768]{2,1,0:T(8,128)(2,1)} custom-call(s32[1,2]{1,0:T(1,128)} %order_ref.3, bf16[1,2,128,4096]{3,2,1,0:T(8,128)(2,1)} %q_ref.1, bf16[1,2,128,8,256]{4,3,2,1,0:T(8,128)(2,1)} %kv_ref.1), custom_call_target="tpu_custom_call" | custom-call | tf_op jit(solution)/shard_map/pack/pallas_call | solution.py:32
  4.8 47.7 %all_to_all.15 = bf16[16,128,768]{2,1,0:T(8,128)(2,1)} all-to-all(bf16[16,128,768]{2,1,0:T(8,128)(2,1)} %pack.1), channel_id=1, replica_groups=mesh['section'=8,'seq'=16] {'seq'}, dimensions={0} | all-to-all | bytes 6291456 | tf_op jit(solution)/shard_map/all_to_all | solution.py:182
  52.5 12.2 %attend.1 = (bf16[2048,256]{1,0:T(8,128)(2,1)}, bf16[2048,256]{1,0:T(8,128)(2,1)}) custom-call(s32[1,2,4]{2,1,0:T(2,128)} %len_ref.1, s32[1,2]{1,0:T(1,128)} %order_ref.3, bf16[2048,768]{1,0:T(8,128)(2,1)} %bitcast.3, bf16[2048,768]{1,0:T(8,128)(2,1)} %bitcast.4), custom_call_target="tpu_custom_call" | custom-call | tf_op jit(solution)/shard_map/attend/pallas_call | solution.py:128
  64.7 3.7 %all-to-all-start.1 = ((bf16[16,128,256]{2,1,0:T(8,128)(2,1)}), bf16[16,128,256]{2,1,0:T(8,128)(2,1)S(1)}, u32[]{:S(2)}, u32[]{:S(2)}) async-start(bf16[16,128,256]{2,1,0:T(8,128)(2,1)} %bitcast.6), calls=%async_computation.1 | async-start | bytes 2097152 | tf_op jit(solution)/shard_map/all_to_all | solution.py:182
  68.4 0.0 collective-permute-start.1
  68.4 16.3 %all-to-all-done.1 = bf16[16,128,256]{2,1,0:T(8,128)(2,1)S(1)} async-done(((bf16[16,128,256]{2,1,0:T(8,128)(2,1)}), bf16[16,128,256]{2,1,0:T(8,128)(2,1)S(1)}, u32[]{:S(2)}, u32[]{:S(2)}) %all-to-all-start.1) | async-done | bytes 1048608 | tf_op jit(solution)/shard_map/all_to_all | solution.py:182
  84.7 0.0 collective-permute-start
  84.7 0.0 collective-permute-done.1
  84.7 0.0 copy-start
  84.7 1.0 copy-done
  85.7 6.6 %all-to-all-start.2 = ((bf16[16,128,256]{2,1,0:T(8,128)(2,1)}), bf16[16,128,256]{2,1,0:T(8,128)(2,1)S(1)}, u32[]{:S(2)}, u32[]{:S(2)}) async-start(bf16[16,128,256]{2,1,0:T(8,128)(2,1)} %bitcast.5), calls=%async_computation.2 | async-start | bytes 2097152 | tf_op jit(solution)/shard_map/all_to_all | solution.py:182
  92.2 7.9 %collective-permute-done.near_ref = bf16[16,128,256]{2,1,0:T(8,128)(2,1)S(1)} collective-permute-done((bf16[16,128,256]{2,1,0:T(8,128)(2,1)S(1)}, bf16[16,128,256]{2,1,0:T(8,128)(2,1)S(1)}, u32[]{:S(2)}, u32[]{:S(2)}) %collective-permute-start) | collective-permute-done | bytes 1048608 | tf_op jit(solution)/shard_map/ppermute | solution.py:192
  100.1 8.5 %all-to-all-done.2.far_ref = bf16[16,128,256]{2,1,0:T(8,128)(2,1)S(1)} async-done(((bf16[16,128,256]{2,1,0:T(8,128)(2,1)}), bf16[16,128,256]{2,1,0:T(8,128)(2,1)S(1)}, u32[]{:S(2)}, u32[]{:S(2)}) %all-to-all-start.2) | async-done | bytes 1048608 | tf_op jit(solution)/shard_map/all_to_all | solution.py:182
  108.6 1.6 %unpack.1 = bf16[1,2,128,4096]{3,2,1,0:T(8,128)(2,1)} custom-call(bf16[16,128,256]{2,1,0:T(8,128)(2,1)S(1)} %collective-permute-done.near_ref, bf16[16,128,256]{2,1,0:T(8,128)(2,1)S(1)} %all-to-all-done.2.far_ref), custom_call_target="tpu_custom_call" | custom-call | tf_op jit(solution)/shard_map/unpack/pallas_call | solution.py:170
Async XLA Ops:
  64.7 20.0 %all-to-all-start.1 = ((bf16[16,128,256]{2,1,0:T(8,128)(2,1)}), bf16[16,128,256]{2,1,0:T(8,128)(2,1)S(1)}, u32[]{:S(2)}, u32[]{:S(2)}) async-start(bf16[16,128,256]{2,1,0:T(8,128)(2,1)} %bitcast.6), calls=%async_computation.1 | async-start | bytes 2097152 | tf_op jit(solution)/shard_map/all_to_all | solution.py:182
  68.4 16.3 %collective-permute-start.1 = (bf16[2048,256]{1,0:T(8,128)(2,1)}, bf16[2048,256]{1,0:T(8,128)(2,1)S(1)}, u32[]{:S(2)}, u32[]{:S(2)}) collective-permute-start(bf16[2048,256]{1,0:T(8,128)(2,1)} %get-tuple-element.8), channel_id=1, source_target_pairs={{0,16},{16,32},{32,48},{48,64},{64,80},{80,96},{96,112},{112,0},{1... | collective-permute-start | bytes 3145736 | tf_op jit(solution)/shard_map/ppermute | solution.py:192
  84.7 15.4 %collective-permute-start = (bf16[16,128,256]{2,1,0:T(8,128)(2,1)S(1)}, bf16[16,128,256]{2,1,0:T(8,128)(2,1)S(1)}, u32[]{:S(2)}, u32[]{:S(2)}) collective-permute-start(bf16[16,128,256]{2,1,0:T(8,128)(2,1)S(1)} %all-to-all-done.1), channel_id=1, source_target_pairs={{0,16},{16,32},{32,48},{48,64},{64,80},{80,96},{96,112},{112,0},{1... | collective-permute-start | bytes 3145736 | tf_op jit(solution)/shard_map/ppermute | solution.py:192
  84.7 1.0 copy-start
  85.7 23.0 %all-to-all-start.2 = ((bf16[16,128,256]{2,1,0:T(8,128)(2,1)}), bf16[16,128,256]{2,1,0:T(8,128)(2,1)S(1)}, u32[]{:S(2)}, u32[]{:S(2)}) async-start(bf16[16,128,256]{2,1,0:T(8,128)(2,1)} %bitcast.5), calls=%async_computation.2 | async-start | bytes 2097152 | tf_op jit(solution)/shard_map/all_to_all | solution.py:182

commit v3 on v2

v3 whole, which is shorter than its diff:
```python
import functools

import jax
import jax.numpy as jnp
from jax import lax
from jax.experimental import pallas as pl
from jax.experimental.pallas import tpu as pltpu
from jax.sharding import PartitionSpec as P

HD = 128
QH = 32
KVH = 8
MB = 2
SHARE = QH // KVH
ROWS = 256
TILE = 128
NEAR = SHARE // 2
EXPONENT = 1.4426950408889634 * HD ** (-0.5)
WINDOWS = 5
GROUP = 32


def pack_kernel(order_ref, q_ref, kv_ref, o_ref, q_buf, kv_buf, pair_buf, q_in, kv_in, q_out, kv_out):
    wide = SHARE * HD
    slots = range(MB)
    loads = []
    for j in slots:
        m = order_ref[0, j]
        kv_load = pltpu.make_async_copy(kv_ref.at[0, m], kv_buf.at[j], kv_in.at[j])
        q_loads = [
            pltpu.make_async_copy(
                q_ref.at[0, m, :, pl.ds(g * wide, wide)], q_buf.at[j, g], q_in.at[j, g]
            )
            for g in range(KVH)
        ]
        loads.append((kv_load, q_loads))
    for kv_load, q_loads in loads:
        kv_load.start()
        for load in q_loads:
            load.start()
    span = GROUP * KVH
    row = lax.broadcasted_iota(jnp.int32, (span, span), 0)
    col = lax.broadcasted_iota(jnp.int32, (span, span), 1)
    source = (row & (GROUP - 1)) * KVH + row // GROUP
    sort = jnp.where(source == col, 1.0, 0.0).astype(jnp.bfloat16)
    stores = []
    for j in slots:
        kv_load, q_loads = loads[j]
        kv_load.wait()
        for t in range(0, kv_buf.shape[1], GROUP):
            mixed = kv_buf[j, t : t + GROUP].reshape(span, 2 * HD)
            split = jnp.dot(sort, mixed, preferred_element_type=jnp.float32).astype(jnp.bfloat16)
            for g in range(KVH):
                pair_buf[j, g, t : t + GROUP, :] = split[g * GROUP : (g + 1) * GROUP]
        for g in range(KVH):
            store = pltpu.make_async_copy(
                pair_buf.at[j, g],
                o_ref.at[j * KVH + g, :, pl.ds(wide, 2 * HD)],
                kv_out.at[j, g],
            )
            store.start()
            stores.append(store)
        for g in range(KVH):
            q_loads[g].wait()
            store = pltpu.make_async_copy(
                q_buf.at[j, g], o_ref.at[j * KVH + g, :, pl.ds(0, wide)], q_out.at[j, g]
            )
            store.start()
            stores.append(store)
    for store in stores:
        store.wait()


def pack(queries, keys_values, order):
    rows = queries.shape[2]
    wide = SHARE * HD
    return pl.pallas_call(
        pack_kernel,
        out_shape=jax.ShapeDtypeStruct((MB * KVH, rows, wide + 2 * HD), jnp.bfloat16),
        in_specs=[
            pl.BlockSpec(memory_space=pltpu.SMEM),
            pl.BlockSpec(memory_space=pl.ANY),
            pl.BlockSpec(memory_space=pl.ANY),
        ],
        out_specs=pl.BlockSpec(memory_space=pl.ANY),
        scratch_shapes=[
            pltpu.VMEM((MB, KVH, rows, wide), jnp.bfloat16),
            pltpu.VMEM((MB, rows, KVH, 2 * HD), jnp.bfloat16),
            pltpu.VMEM((MB, KVH, rows, 2 * HD), jnp.bfloat16),
            pltpu.SemaphoreType.DMA((MB, KVH)),
            pltpu.SemaphoreType.DMA((MB,)),
            pltpu.SemaphoreType.DMA((MB, KVH)),
            pltpu.SemaphoreType.DMA((MB, KVH)),
        ],
        name="pack",
    )(order, queries, keys_values)


def attend_kernel(
    len_ref, order_ref, x_ref, near_ref, far_ref, ve_ref, s_ref, m_ref, o_ref, sems
):
    m = order_ref[0, lax.axis_index("seq") // KVH]
    wide = SHARE * HD
    tokens = x_ref.shape[0]
    steps = tokens // ROWS
    ve_ref[:, 0:HD] = x_ref[:, wide + HD : wide + 2 * HD]
    ve_ref[:, HD : 2 * HD] = jnp.ones((tokens, HD), jnp.bfloat16)

    end0 = len_ref[0, m, 0]
    end1 = end0 + len_ref[0, m, 1]
    end2 = end1 + len_ref[0, m, 2]

    def start_of(t):
        late = jnp.where(t < end1, end0, jnp.where(t < end2, end1, end2))
        return jnp.where(t < end0, 0, late)

    lane = lax.broadcasted_iota(jnp.int32, (ROWS, TILE), 1)
    pair = 2
    last = ROWS // TILE
    outs = (near_ref, far_ref)

    def copy_out(g, i):
        rows = pl.ds(pl.multiple_of(i * ROWS, ROWS), ROWS)
        return pltpu.make_async_copy(o_ref.at[g, i], outs[g].at[rows, :], sems.at[g, i])

    def block(i, carry):
        row0 = pl.multiple_of(i * ROWS, ROWS)
        need = i + 1 - start_of(row0) // ROWS
        token = row0 + lax.broadcasted_iota(jnp.int32, (ROWS, TILE), 0)
        begin = start_of(token)

        def window(n):
            low = pl.multiple_of((i + 1 - n) * ROWS, ROWS)
            tiles = n * ROWS // TILE

            def score(g):
                heads = range(g * pair, (g + 1) * pair)
                q = jnp.concatenate(
                    [x_ref[pl.ds(row0, ROWS), h * HD : (h + 1) * HD] for h in heads], axis=0
                )
                scores = lax.dot_general(
                    q,
                    x_ref[pl.ds(low, n * ROWS), wide : wide + HD],
                    (((1,), (1,)), ((), ())),
                    preferred_element_type=jnp.float32,
                )
                top = None
                for j in range(tiles):
                    key = low + j * TILE + lane
                    allowed = key >= begin
                    if j >= tiles - last:
                        allowed = allowed & (key <= token)
                    allowed = jnp.concatenate([allowed] * pair, axis=0)
                    tile = jnp.where(allowed, scores[:, j * TILE : (j + 1) * TILE], -jnp.inf)
                    s_ref[g, :, j * TILE : (j + 1) * TILE] = tile
                    top = tile if top is None else jnp.maximum(top, tile)
                peak = jnp.max(top, axis=1, keepdims=True)
                m_ref[g] = jnp.broadcast_to(peak, (pair * ROWS, TILE))

            def mix(g):
                peak = m_ref[g]
                weights = [
                    jnp.exp2(
                        (s_ref[g, :, j * TILE : (j + 1) * TILE] - peak) * EXPONENT
                    ).astype(jnp.bfloat16)
                    for j in range(tiles)
                ]
                mixed = jnp.dot(
                    jnp.concatenate(weights, axis=1),
                    ve_ref[pl.ds(low, n * ROWS), :],
                    preferred_element_type=jnp.float32,
                )
                out = (mixed[:, 0:HD] / mixed[:, HD : 2 * HD]).astype(jnp.bfloat16)
                for h in range(pair):
                    o_ref[g, i, :, h * HD : (h + 1) * HD] = out[h * ROWS : (h + 1) * ROWS, :]

            score(0)
            score(1)
            mix(0)
            mix(1)

        for n in range(1, WINDOWS + 1):
            pl.when(need == n)(functools.partial(window, n))
        for g in range(2):
            copy_out(g, i).start()
        return carry

    lax.fori_loop(0, steps, block, 0)
    for g in range(2):
        for i in range(steps):
            copy_out(g, i).wait()


def attend(packed, lengths, order):
    tokens = packed.shape[0]
    half = NEAR * HD
    steps = tokens // ROWS
    return pl.pallas_call(
        attend_kernel,
        out_shape=[jax.ShapeDtypeStruct((tokens, half), jnp.bfloat16)] * 2,
        in_specs=[
            pl.BlockSpec(memory_space=pltpu.SMEM),
            pl.BlockSpec(memory_space=pltpu.SMEM),
            pl.BlockSpec(memory_space=pltpu.VMEM),
        ],
        out_specs=[pl.BlockSpec(memory_space=pl.ANY)] * 2,
        scratch_shapes=[
            pltpu.VMEM((tokens, 2 * HD), jnp.bfloat16),
            pltpu.VMEM((2, NEAR * ROWS, WINDOWS * ROWS), jnp.float32),
            pltpu.VMEM((2, NEAR * ROWS, TILE), jnp.float32),
            pltpu.VMEM((2, steps, ROWS, half), jnp.bfloat16),
            pltpu.SemaphoreType.DMA((2, steps)),
        ],
        compiler_params=pltpu.CompilerParams(vmem_limit_bytes=32 << 20),
        name="attend",
    )(lengths, order, packed)


def unpack_kernel(near_ref, far_ref, o_ref, sems):
    copies = []
    for k in range(MB * KVH):
        for p, ref in enumerate((near_ref, far_ref)):
            part = ref.shape[2]
            col = (k % KVH) * SHARE * HD + p * part
            copies.append(
                pltpu.make_async_copy(
                    ref.at[k], o_ref.at[0, k // KVH, :, pl.ds(col, part)], sems.at[p, k]
                )
            )
    for copy in copies:
        copy.start()
    for copy in copies:
        copy.wait()


def unpack(near, far):
    rows = near.shape[1]
    return pl.pallas_call(
        unpack_kernel,
        out_shape=jax.ShapeDtypeStruct((1, MB, rows, QH * HD), jnp.bfloat16),
        in_specs=[pl.BlockSpec(memory_space=pltpu.VMEM)] * 2,
        out_specs=pl.BlockSpec(memory_space=pl.ANY),
        scratch_shapes=[pltpu.SemaphoreType.DMA((2, MB * KVH))],
        compiler_params=pltpu.CompilerParams(vmem_limit_bytes=8 << 20),
        name="unpack",
    )(near, far)


def exchange(blocks):
    return lax.all_to_all(blocks, "seq", split_axis=0, concat_axis=0, tiled=True)


def handed_on(block):
    sections = lax.axis_size("section")
    return lax.ppermute(block, "section", [(i, (i + 1) % sections) for i in range(sections)])


def handed_on(block):
    sections = lax.axis_size("section")
    return lax.ppermute(block, "section", [(i, (i + 1) % sections) for i in range(sections)])


def local(queries, keys_values, lengths, order):
    n_seq = MB * KVH
    rows = queries.shape[2]
    packed = exchange(pack(queries, keys_values, order)).reshape(n_seq * rows, -1)
    near, far = attend(packed, lengths, order)
    far = handed_on(far)
    near = handed_on(exchange(near.reshape(n_seq, rows, -1)))
    far = exchange(far.reshape(n_seq, rows, -1))
    return unpack(near, far)


def solution(mesh):
    placed = (
        P("section", None, "seq", None),
        P("section", None, "seq", None, None),
        P("section", None, None),
        P("section", None),
    )
    return jax.shard_map(
        local,
        mesh=mesh,
        in_specs=placed,
        out_specs=P("section", None, "seq", None),
        check_vma=False,
    )
```

time: 111 us -> 109 us (0.982)
  transfers between devices with their start and end apart: 4 -> 4, of which waited for: 3 -> 4; matrix products, arithmetic and copies ran while one was open for 0% -> 0% of each run, Pallas kernels for 0% -> 0%
where the time goes in v3:
time: 109 us
  blocking collectives  47.6 us (44%)
  waiting for transfers between devices  32.5 us (30%)
  Pallas kernels  18 us (17%)
  starting transfers between devices  10.8 us (10%)
    all_to_all x1, blocking collectives, exchange(): lax.all_to_all(blocks, 'seq', split_axis=0, concat_axis=0, tiled=True)  47.6 us
    all_to_all x2, waiting for transfers between devices, exchange(): lax.all_to_all(blocks, 'seq', split_axis=0, concat_axis=0, tiled=True)  24.2 us
    pallas_call x1, Pallas kernels, attend(): pl.pallas_call(attend_kernel, out_shape=[jax.ShapeDtypeStruct((tokens, ha...  11.7 us
    all_to_all x2, starting transfers between devices, exchange(): lax.all_to_all(blocks, 'seq', split_axis=0, concat_axis=0, tiled=True)  10.8 us
    ppermute x2, waiting for transfers between devices, handed_on(): lax.ppermute(block, 'section', [(i, (i + 1) % sections) for i in range(se...  8.28 us
    pallas_call x1, Pallas kernels, pack(): pl.pallas_call(pack_kernel, out_shape=jax.ShapeDtypeStruct((MB * KVH, row...  4.78 us
  transfers between devices with their start and end apart: 4, of which 4 were waited for; matrix products, arithmetic and copies ran while one was open for 0% of the time, Pallas kernels for 0%

profile of v3, /device:TPU:0, one launch (start us, length us, event | category | flops | bytes accessed | tf_op | source)
XLA Modules:
  0.0 109.1 jit_solution(7554757242622743002)
XLA Ops:
  0.0 4.8 %pack.1 = bf16[16,128,768]{2,1,0:T(8,128)(2,1)} custom-call(s32[1,2]{1,0:T(1,128)} %order_ref.3, bf16[1,2,128,4096]{3,2,1,0:T(8,128)(2,1)} %q_ref.1, bf16[1,2,128,8,256]{4,3,2,1,0:T(8,128)(2,1)} %kv_ref.1), custom_call_target="tpu_custom_call" | custom-call | tf_op jit(solution)/shard_map/pack/pallas_call | solution.py:77
  4.8 0.0 copy-start
  4.8 0.0 copy-start.1
  4.8 47.6 %all_to_all.15 = bf16[16,128,768]{2,1,0:T(8,128)(2,1)S(1)} all-to-all(bf16[16,128,768]{2,1,0:T(8,128)(2,1)} %pack.1), channel_id=1, replica_groups=mesh['section'=8,'seq'=16] {'seq'}, dimensions={0} | all-to-all | bytes 6291456 | tf_op jit(solution)/shard_map/all_to_all | solution.py:250
  52.4 0.0 copy-done
  52.4 0.0 copy-done.1
  52.4 11.7 %attend.1 = (bf16[2048,256]{1,0:T(8,128)(2,1)}, bf16[2048,256]{1,0:T(8,128)(2,1)S(1)}) custom-call(s32[1,2,4]{2,1,0:T(2,128)S(1)} %copy-done.1, s32[1,2]{1,0:T(1,128)S(1)} %copy-done, bf16[2048,768]{1,0:T(8,128)(2,1)S(1)} %bitcast.3), custom_call_target="tpu_custom_call" | custom-call | tf_op jit(solution)/shard_map/attend/pallas_call | solution.py:198
  64.1 3.7 %all-to-all-start.1 = ((bf16[16,128,256]{2,1,0:T(8,128)(2,1)}), bf16[16,128,256]{2,1,0:T(8,128)(2,1)S(1)}, u32[]{:S(2)}, u32[]{:S(2)}) async-start(bf16[16,128,256]{2,1,0:T(8,128)(2,1)} %bitcast.1), calls=%async_computation.1 | async-start | bytes 2097152 | tf_op jit(solution)/shard_map/all_to_all | solution.py:250
  67.8 0.0 collective-permute-start.1
  67.8 15.3 %all-to-all-done.1 = bf16[16,128,256]{2,1,0:T(8,128)(2,1)S(1)} async-done(((bf16[16,128,256]{2,1,0:T(8,128)(2,1)}), bf16[16,128,256]{2,1,0:T(8,128)(2,1)S(1)}, u32[]{:S(2)}, u32[]{:S(2)}) %all-to-all-start.1) | async-done | bytes 1048608 | tf_op jit(solution)/shard_map/all_to_all | solution.py:250
  83.1 0.0 collective-permute-start
  83.1 0.2 collective-permute-done.1
  83.3 7.1 %all-to-all-start.2 = ((bf16[16,128,256]{2,1,0:T(8,128)(2,1)}), bf16[16,128,256]{2,1,0:T(8,128)(2,1)S(1)}, u32[]{:S(2)}, u32[]{:S(2)}) async-start(bf16[16,128,256]{2,1,0:T(8,128)(2,1)} %bitcast.2), calls=%async_computation.2 | async-start | bytes 2097152 | tf_op jit(solution)/shard_map/all_to_all | solution.py:250
  90.5 8.1 %collective-permute-done.near_ref = bf16[16,128,256]{2,1,0:T(8,128)(2,1)S(1)} collective-permute-done((bf16[16,128,256]{2,1,0:T(8,128)(2,1)S(1)}, bf16[16,128,256]{2,1,0:T(8,128)(2,1)S(1)}, u32[]{:S(2)}, u32[]{:S(2)}) %collective-permute-start) | collective-permute-done | bytes 1048608 | tf_op jit(solution)/shard_map/ppermute | solution.py:260
  98.6 8.9 %all-to-all-done.2.far_ref = bf16[16,128,256]{2,1,0:T(8,128)(2,1)S(1)} async-done(((bf16[16,128,256]{2,1,0:T(8,128)(2,1)}), bf16[16,128,256]{2,1,0:T(8,128)(2,1)S(1)}, u32[]{:S(2)}, u32[]{:S(2)}) %all-to-all-start.2) | async-done | bytes 1048608 | tf_op jit(solution)/shard_map/all_to_all | solution.py:250
  107.5 1.6 %unpack.1 = bf16[1,2,128,4096]{3,2,1,0:T(8,128)(2,1)} custom-call(bf16[16,128,256]{2,1,0:T(8,128)(2,1)S(1)} %collective-permute-done.near_ref, bf16[16,128,256]{2,1,0:T(8,128)(2,1)S(1)} %all-to-all-done.2.far_ref), custom_call_target="tpu_custom_call" | custom-call | tf_op jit(solution)/shard_map/unpack/pallas_call | solution.py:238
Async XLA Ops:
  4.8 47.6 %copy-start = (s32[1,2]{1,0:T(1,128)S(1)}, s32[1,2]{1,0:T(1,128)}, u32[]{:S(2)}) copy-start(s32[1,2]{1,0:T(1,128)} %order_ref.3) | copy-start | bytes 28
  4.8 47.6 %copy-start.1 = (s32[1,2,4]{2,1,0:T(2,128)S(1)}, s32[1,2,4]{2,1,0:T(2,128)}, u32[]{:S(2)}) copy-start(s32[1,2,4]{2,1,0:T(2,128)} %len_ref.1) | copy-start | bytes 100
  64.1 19.0 %all-to-all-start.1 = ((bf16[16,128,256]{2,1,0:T(8,128)(2,1)}), bf16[16,128,256]{2,1,0:T(8,128)(2,1)S(1)}, u32[]{:S(2)}, u32[]{:S(2)}) async-start(bf16[16,128,256]{2,1,0:T(8,128)(2,1)} %bitcast.1), calls=%async_computation.1 | async-start | bytes 2097152 | tf_op jit(solution)/shard_map/all_to_all | solution.py:250
  67.8 15.6 %collective-permute-start.1 = (bf16[2048,256]{1,0:T(8,128)(2,1)S(1)}, bf16[2048,256]{1,0:T(8,128)(2,1)}, u32[]{:S(2)}, u32[]{:S(2)}) collective-permute-start(bf16[2048,256]{1,0:T(8,128)(2,1)S(1)} %get-tuple-element.8), channel_id=1, source_target_pairs={{0,16},{16,32},{32,48},{48,64},{64,80},{80,96},{96,112},{112,0},{1... | collective-permute-start | bytes 3145736 | tf_op jit(solution)/shard_map/ppermute | solution.py:260
  83.1 15.4 %collective-permute-start = (bf16[16,128,256]{2,1,0:T(8,128)(2,1)S(1)}, bf16[16,128,256]{2,1,0:T(8,128)(2,1)S(1)}, u32[]{:S(2)}, u32[]{:S(2)}) collective-permute-start(bf16[16,128,256]{2,1,0:T(8,128)(2,1)S(1)} %all-to-all-done.1), channel_id=1, source_target_pairs={{0,16},{16,32},{32,48},{48,64},{64,80},{80,96},{96,112},{112,0},{1... | collective-permute-start | bytes 3145736 | tf_op jit(solution)/shard_map/ppermute | solution.py:260
  83.3 24.1 %all-to-all-start.2 = ((bf16[16,128,256]{2,1,0:T(8,128)(2,1)}), bf16[16,128,256]{2,1,0:T(8,128)(2,1)S(1)}, u32[]{:S(2)}, u32[]{:S(2)}) async-start(bf16[16,128,256]{2,1,0:T(8,128)(2,1)} %bitcast.2), calls=%async_computation.2 | async-start | bytes 2097152 | tf_op jit(solution)/shard_map/all_to_all | solution.py:250

commit v4 on v3

--- a/solution.py
+++ b/solution.py
@@ -6,6 +6,7 @@
 from jax.experimental import pallas as pl
 from jax.experimental.pallas import tpu as pltpu
 from jax.sharding import PartitionSpec as P
+
 
 HD = 128
 QH = 32
@@ -114,81 +115,88 @@
         late = jnp.where(t < end1, end0, jnp.where(t < end2, end1, end2))
         return jnp.where(t < end0, 0, late)
 
-    lane = lax.broadcasted_iota(jnp.int32, (ROWS, TILE), 1)
-    pair = 2
-    last = ROWS // TILE
+    row = lax.broadcasted_iota(jnp.int32, (TILE, TILE), 0)
+    lane = lax.broadcasted_iota(jnp.int32, (TILE, TILE), 1)
+    diagonal = lane <= row
+    halves = ROWS // TILE
     outs = (near_ref, far_ref)
 
-    def copy_out(g, i):
+    def copy_out(h, i):
         rows = pl.ds(pl.multiple_of(i * ROWS, ROWS), ROWS)
-        return pltpu.make_async_copy(o_ref.at[g, i], outs[g].at[rows, :], sems.at[g, i])
+        cols = pl.ds((h % NEAR) * HD, HD)
+        return pltpu.make_async_copy(
+            o_ref.at[h, i], outs[h // NEAR].at[rows, cols], sems.at[h, i]
+        )
 
     def block(i, carry):
         row0 = pl.multiple_of(i * ROWS, ROWS)
         need = i + 1 - start_of(row0) // ROWS
-        token = row0 + lax.broadcasted_iota(jnp.int32, (ROWS, TILE), 0)
-        begin = start_of(token)
+        begins = [start_of(row0 + k * TILE + row) for k in range(halves)]
 
         def window(n):
             low = pl.multiple_of((i + 1 - n) * ROWS, ROWS)
-            tiles = n * ROWS // TILE
-
-            def score(g):
-                heads = range(g * pair, (g + 1) * pair)
-                q = jnp.concatenate(
-                    [x_ref[pl.ds(row0, ROWS), h * HD : (h + 1) * HD] for h in heads], axis=0
-                )
+
+            def tiles(k):
+                return (n - 1) * halves + k + 1
+
+            def score(h):
                 scores = lax.dot_general(
-                    q,
+                    x_ref[pl.ds(row0, ROWS), h * HD : (h + 1) * HD],
                     x_ref[pl.ds(low, n * ROWS), wide : wide + HD],
                     (((1,), (1,)), ((), ())),
                     preferred_element_type=jnp.float32,
                 )
-                top = None
-                for j in range(tiles):
-                    key = low + j * TILE + lane
-                    allowed = key >= begin
-                    if j >= tiles - last:
-                        allowed = allowed & (key <= token)
-                    allowed = jnp.concatenate([allowed] * pair, axis=0)
-                    tile = jnp.where(allowed, scores[:, j * TILE : (j + 1) * TILE], -jnp.inf)
-                    s_ref[g, :, j * TILE : (j + 1) * TILE] = tile
-                    top = tile if top is None else jnp.maximum(top, tile)
-                peak = jnp.max(top, axis=1, keepdims=True)
-                m_ref[g] = jnp.broadcast_to(peak, (pair * ROWS, TILE))
-
-            def mix(g):
-                peak = m_ref[g]
-                weights = [
-                    jnp.exp2(
-                        (s_ref[g, :, j * TILE : (j + 1) * TILE] - peak) * EXPONENT
-                    ).astype(jnp.bfloat16)
-                    for j in range(tiles)
-                ]
+                for k in range(halves):
+                    rows = slice(k * TILE, (k + 1) * TILE)
+                    top = None
+                    for j in range(tiles(k)):
+                        allowed = low + j * TILE + lane >= begins[k]
+                        if j == tiles(k) - 1:
+                            allowed = allowed & diagonal
+                        tile = jnp.where(
+                            allowed, scores[rows, j * TILE : (j + 1) * TILE], -jnp.inf
+                        )
+                        s_ref[h % 2, rows, j * TILE : (j + 1) * TILE] = tile
+                        top = tile if top is None else jnp.maximum(top, tile)
+                    peak = jnp.max(top, axis=1, keepdims=True)
+                    m_ref[h % 2, rows, :] = jnp.broadcast_to(peak, (TILE, TILE))
+
+            def mix(h):
+                strips = []
+                for k in range(halves):
+                    rows = slice(k * TILE, (k + 1) * TILE)
+                    peak = m_ref[h % 2, rows, :]
+                    strip = [
+                        jnp.exp2(
+                            (s_ref[h % 2, rows, j * TILE : (j + 1) * TILE] - peak) * EXPONENT
+                        ).astype(jnp.bfloat16)
+                        for j in range(tiles(k))
+                    ]
+                    strip += [jnp.zeros((TILE, TILE), jnp.bfloat16)] * (n * halves - tiles(k))
+                    strips.append(jnp.concatenate(strip, axis=1))
                 mixed = jnp.dot(
-                    jnp.concatenate(weights, axis=1),
+                    jnp.concatenate(strips, axis=0),
                     ve_ref[pl.ds(low, n * ROWS), :],
                     preferred_element_type=jnp.float32,
                 )
-                out = (mixed[:, 0:HD] / mixed[:, HD : 2 * HD]).astype(jnp.bfloat16)
-                for h in range(pair):
-                    o_ref[g, i, :, h * HD : (h + 1) * HD] = out[h * ROWS : (h + 1) * ROWS, :]
+                o_ref[h, i] = (mixed[:, 0:HD] / mixed[:, HD : 2 * HD]).astype(jnp.bfloat16)
 
             score(0)
-            score(1)
-            mix(0)
-            mix(1)
+            for h in range(SHARE - 1):
+                mix(h)
+                score(h + 1)
+            mix(SHARE - 1)
 
         for n in range(1, WINDOWS + 1):
             pl.when(need == n)(functools.partial(window, n))
-        for g in range(2):
-            copy_out(g, i).start()
+        for h in range(SHARE):
+            copy_out(h, i).start()
         return carry
 
     lax.fori_loop(0, steps, block, 0)
-    for g in range(2):
+    for h in range(SHARE):
         for i in range(steps):
-            copy_out(g, i).wait()
+            copy_out(h, i).wait()
 
 
 def attend(packed, lengths, order):
@@ -206,10 +214,10 @@
         out_specs=[pl.BlockSpec(memory_space=pl.ANY)] * 2,
         scratch_shapes=[
             pltpu.VMEM((tokens, 2 * HD), jnp.bfloat16),
-            pltpu.VMEM((2, NEAR * ROWS, WINDOWS * ROWS), jnp.float32),
-            pltpu.VMEM((2, NEAR * ROWS, TILE), jnp.float32),
-            pltpu.VMEM((2, steps, ROWS, half), jnp.bfloat16),
-            pltpu.SemaphoreType.DMA((2, steps)),
+            pltpu.VMEM((2, ROWS, WINDOWS * ROWS), jnp.float32),
+            pltpu.VMEM((2, ROWS, TILE), jnp.float32),
+            pltpu.VMEM((SHARE, steps, ROWS, HD), jnp.bfloat16),
+            pltpu.SemaphoreType.DMA((SHARE, steps)),
         ],
         compiler_params=pltpu.CompilerParams(vmem_limit_bytes=32 << 20),
         name="attend",
@@ -266,7 +274,8 @@
     packed = exchange(pack(queries, keys_values, order)).reshape(n_seq * rows, -1)
     near, far = attend(packed, lengths, order)
     far = handed_on(far)
-    near = handed_on(exchange(near.reshape(n_seq, rows, -1)))
+    near = exchange(near.reshape(n_seq, rows, -1))
+    near = handed_on(near)
     far = exchange(far.reshape(n_seq, rows, -1))
     return unpack(near, far)
 

time: 109 us -> 110 us (level)
  Pallas kernels: 18 us -> 19.3 us
    pallas_call x1, Pallas kernels: 11.7 us -> 12.9 us  [attend(): pl.pallas_call(attend_kernel, out_shape=[jax.ShapeDtypeStruct((tokens, ha...]
where the time goes in v4:
time: 110 us; the launch traced here: 109 us
  blocking collectives  47.6 us (43%)
  waiting for transfers between devices  31.5 us (29%)
  Pallas kernels  19.3 us (18%)
  starting transfers between devices  10.8 us (10%)
    all_to_all x1, blocking collectives, exchange(): lax.all_to_all(blocks, 'seq', split_axis=0, concat_axis=0, tiled=True)  47.6 us
    all_to_all x2, waiting for transfers between devices, exchange(): lax.all_to_all(blocks, 'seq', split_axis=0, concat_axis=0, tiled=True)  23.2 us
    pallas_call x1, Pallas kernels, attend(): pl.pallas_call(attend_kernel, out_shape=[jax.ShapeDtypeStruct((tokens, ha...  12.9 us
    all_to_all x2, starting transfers between devices, exchange(): lax.all_to_all(blocks, 'seq', split_axis=0, concat_axis=0, tiled=True)  10.8 us
    ppermute x2, waiting for transfers between devices, handed_on(): lax.ppermute(block, 'section', [(i, (i + 1) % sections) for i in range(se...  8.28 us
    pallas_call x1, Pallas kernels, pack(): pl.pallas_call(pack_kernel, out_shape=jax.ShapeDtypeStruct((MB * KVH, row...  4.78 us
  transfers between devices with their start and end apart: 4, of which 4 were waited for; matrix products, arithmetic and copies ran while one was open for 0% of the time, Pallas kernels for 0%

profile of v4, /device:TPU:0, one launch (start us, length us, event | category | flops | bytes accessed | tf_op | source)
XLA Modules:
  0.0 109.3 jit_solution(385943844131720455)
XLA Ops:
  0.0 4.8 %pack.1 = bf16[16,128,768]{2,1,0:T(8,128)(2,1)} custom-call(s32[1,2]{1,0:T(1,128)} %order_ref.3, bf16[1,2,128,4096]{3,2,1,0:T(8,128)(2,1)} %q_ref.1, bf16[1,2,128,8,256]{4,3,2,1,0:T(8,128)(2,1)} %kv_ref.1), custom_call_target="tpu_custom_call" | custom-call | tf_op jit(solution)/shard_map/pack/pallas_call | solution.py:78
  4.8 0.0 copy-start
  4.8 0.0 copy-start.1
  4.8 47.6 %all_to_all.15 = bf16[16,128,768]{2,1,0:T(8,128)(2,1)S(1)} all-to-all(bf16[16,128,768]{2,1,0:T(8,128)(2,1)} %pack.1), channel_id=1, replica_groups=mesh['section'=8,'seq'=16] {'seq'}, dimensions={0} | all-to-all | bytes 6291456 | tf_op jit(solution)/shard_map/all_to_all | solution.py:258
  52.4 0.0 copy-done
  52.4 0.0 copy-done.1
  52.4 12.9 %attend.1 = (bf16[2048,256]{1,0:T(8,128)(2,1)}, bf16[2048,256]{1,0:T(8,128)(2,1)S(1)}) custom-call(s32[1,2,4]{2,1,0:T(2,128)S(1)} %copy-done.1, s32[1,2]{1,0:T(1,128)S(1)} %copy-done, bf16[2048,768]{1,0:T(8,128)(2,1)S(1)} %bitcast.3), custom_call_target="tpu_custom_call" | custom-call | tf_op jit(solution)/shard_map/attend/pallas_call | solution.py:206
  65.4 3.7 %all-to-all-start.1 = ((bf16[16,128,256]{2,1,0:T(8,128)(2,1)}), bf16[16,128,256]{2,1,0:T(8,128)(2,1)S(1)}, u32[]{:S(2)}, u32[]{:S(2)}) async-start(bf16[16,128,256]{2,1,0:T(8,128)(2,1)} %bitcast.1), calls=%async_computation.1 | async-start | bytes 2097152 | tf_op jit(solution)/shard_map/all_to_all | solution.py:258
  69.0 0.0 collective-permute-start.1
  69.1 14.9 %all-to-all-done.1 = bf16[16,128,256]{2,1,0:T(8,128)(2,1)S(1)} async-done(((bf16[16,128,256]{2,1,0:T(8,128)(2,1)}), bf16[16,128,256]{2,1,0:T(8,128)(2,1)S(1)}, u32[]{:S(2)}, u32[]{:S(2)}) %all-to-all-start.1) | async-done | bytes 1048608 | tf_op jit(solution)/shard_map/all_to_all | solution.py:258
  84.0 0.0 collective-permute-start
  84.0 0.6 collective-permute-done.1
  84.6 7.1 %all-to-all-start.2 = ((bf16[16,128,256]{2,1,0:T(8,128)(2,1)}), bf16[16,128,256]{2,1,0:T(8,128)(2,1)S(1)}, u32[]{:S(2)}, u32[]{:S(2)}) async-start(bf16[16,128,256]{2,1,0:T(8,128)(2,1)} %bitcast.2), calls=%async_computation.2 | async-start | bytes 2097152 | tf_op jit(solution)/shard_map/all_to_all | solution.py:258
  91.7 7.7 %collective-permute-done.near_ref = bf16[16,128,256]{2,1,0:T(8,128)(2,1)S(1)} collective-permute-done((bf16[16,128,256]{2,1,0:T(8,128)(2,1)S(1)}, bf16[16,128,256]{2,1,0:T(8,128)(2,1)S(1)}, u32[]{:S(2)}, u32[]{:S(2)}) %collective-permute-start) | collective-permute-done | bytes 1048608 | tf_op jit(solution)/shard_map/ppermute | solution.py:268
  99.4 8.3 %all-to-all-done.2.far_ref = bf16[16,128,256]{2,1,0:T(8,128)(2,1)S(1)} async-done(((bf16[16,128,256]{2,1,0:T(8,128)(2,1)}), bf16[16,128,256]{2,1,0:T(8,128)(2,1)S(1)}, u32[]{:S(2)}, u32[]{:S(2)}) %all-to-all-start.2) | async-done | bytes 1048608 | tf_op jit(solution)/shard_map/all_to_all | solution.py:258
  107.7 1.6 %unpack.1 = bf16[1,2,128,4096]{3,2,1,0:T(8,128)(2,1)} custom-call(bf16[16,128,256]{2,1,0:T(8,128)(2,1)S(1)} %collective-permute-done.near_ref, bf16[16,128,256]{2,1,0:T(8,128)(2,1)S(1)} %all-to-all-done.2.far_ref), custom_call_target="tpu_custom_call" | custom-call | tf_op jit(solution)/shard_map/unpack/pallas_call | solution.py:246
Async XLA Ops:
  4.8 47.6 %copy-start = (s32[1,2]{1,0:T(1,128)S(1)}, s32[1,2]{1,0:T(1,128)}, u32[]{:S(2)}) copy-start(s32[1,2]{1,0:T(1,128)} %order_ref.3) | copy-start | bytes 28
  4.8 47.6 %copy-start.1 = (s32[1,2,4]{2,1,0:T(2,128)S(1)}, s32[1,2,4]{2,1,0:T(2,128)}, u32[]{:S(2)}) copy-start(s32[1,2,4]{2,1,0:T(2,128)} %len_ref.1) | copy-start | bytes 100
  65.4 18.6 %all-to-all-start.1 = ((bf16[16,128,256]{2,1,0:T(8,128)(2,1)}), bf16[16,128,256]{2,1,0:T(8,128)(2,1)S(1)}, u32[]{:S(2)}, u32[]{:S(2)}) async-start(bf16[16,128,256]{2,1,0:T(8,128)(2,1)} %bitcast.1), calls=%async_computation.1 | async-start | bytes 2097152 | tf_op jit(solution)/shard_map/all_to_all | solution.py:258
  69.0 15.6 %collective-permute-start.1 = (bf16[2048,256]{1,0:T(8,128)(2,1)S(1)}, bf16[2048,256]{1,0:T(8,128)(2,1)}, u32[]{:S(2)}, u32[]{:S(2)}) collective-permute-start(bf16[2048,256]{1,0:T(8,128)(2,1)S(1)} %get-tuple-element.8), channel_id=1, source_target_pairs={{0,16},{16,32},{32,48},{48,64},{64,80},{80,96},{96,112},{112,0},{1... | collective-permute-start | bytes 3145736 | tf_op jit(solution)/shard_map/ppermute | solution.py:268
  84.0 15.4 %collective-permute-start = (bf16[16,128,256]{2,1,0:T(8,128)(2,1)S(1)}, bf16[16,128,256]{2,1,0:T(8,128)(2,1)S(1)}, u32[]{:S(2)}, u32[]{:S(2)}) collective-permute-start(bf16[16,128,256]{2,1,0:T(8,128)(2,1)S(1)} %all-to-all-done.1), channel_id=1, source_target_pairs={{0,16},{16,32},{32,48},{48,64},{64,80},{80,96},{96,112},{112,0},{1... | collective-permute-start | bytes 3145736 | tf_op jit(solution)/shard_map/ppermute | solution.py:268
  84.6 23.1 %all-to-all-start.2 = ((bf16[16,128,256]{2,1,0:T(8,128)(2,1)}), bf16[16,128,256]{2,1,0:T(8,128)(2,1)S(1)}, u32[]{:S(2)}, u32[]{:S(2)}) async-start(bf16[16,128,256]{2,1,0:T(8,128)(2,1)} %bitcast.2), calls=%async_computation.2 | async-start | bytes 2097152 | tf_op jit(solution)/shard_map/all_to_all | solution.py:258

commit v5 on v3

--- a/solution.py
+++ b/solution.py
@@ -6,6 +6,7 @@
 from jax.experimental import pallas as pl
 from jax.experimental.pallas import tpu as pltpu
 from jax.sharding import PartitionSpec as P
+
 
 HD = 128
 QH = 32
@@ -20,55 +21,39 @@
 GROUP = 32
 
 
-def pack_kernel(order_ref, q_ref, kv_ref, o_ref, q_buf, kv_buf, pair_buf, q_in, kv_in, q_out, kv_out):
+def pack_kernel(order_ref, q_ref, kv_ref, o_ref, kv_buf, q_in, kv_in):
     wide = SHARE * HD
     slots = range(MB)
-    loads = []
+    kv_loads, q_loads = [], []
     for j in slots:
         m = order_ref[0, j]
-        kv_load = pltpu.make_async_copy(kv_ref.at[0, m], kv_buf.at[j], kv_in.at[j])
-        q_loads = [
+        kv_loads.append(pltpu.make_async_copy(kv_ref.at[0, m], kv_buf.at[j], kv_in.at[j]))
+        q_loads += [
             pltpu.make_async_copy(
-                q_ref.at[0, m, :, pl.ds(g * wide, wide)], q_buf.at[j, g], q_in.at[j, g]
+                q_ref.at[0, m, :, pl.ds(g * wide, wide)],
+                o_ref.at[j * KVH + g, :, pl.ds(0, wide)],
+                q_in.at[j, g],
             )
             for g in range(KVH)
         ]
-        loads.append((kv_load, q_loads))
-    for kv_load, q_loads in loads:
-        kv_load.start()
-        for load in q_loads:
-            load.start()
+    for load in kv_loads + q_loads:
+        load.start()
     span = GROUP * KVH
     row = lax.broadcasted_iota(jnp.int32, (span, span), 0)
     col = lax.broadcasted_iota(jnp.int32, (span, span), 1)
     source = (row & (GROUP - 1)) * KVH + row // GROUP
     sort = jnp.where(source == col, 1.0, 0.0).astype(jnp.bfloat16)
-    stores = []
     for j in slots:
-        kv_load, q_loads = loads[j]
-        kv_load.wait()
+        kv_loads[j].wait()
         for t in range(0, kv_buf.shape[1], GROUP):
             mixed = kv_buf[j, t : t + GROUP].reshape(span, 2 * HD)
             split = jnp.dot(sort, mixed, preferred_element_type=jnp.float32).astype(jnp.bfloat16)
             for g in range(KVH):
-                pair_buf[j, g, t : t + GROUP, :] = split[g * GROUP : (g + 1) * GROUP]
-        for g in range(KVH):
-            store = pltpu.make_async_copy(
-                pair_buf.at[j, g],
-                o_ref.at[j * KVH + g, :, pl.ds(wide, 2 * HD)],
-                kv_out.at[j, g],
-            )
-            store.start()
-            stores.append(store)
-        for g in range(KVH):
-            q_loads[g].wait()
-            store = pltpu.make_async_copy(
-                q_buf.at[j, g], o_ref.at[j * KVH + g, :, pl.ds(0, wide)], q_out.at[j, g]
-            )
-            store.start()
-            stores.append(store)
-    for store in stores:
-        store.wait()
+                o_ref[j * KVH + g, t : t + GROUP, wide : wide + 2 * HD] = split[
+                    g * GROUP : (g + 1) * GROUP
+                ]
+    for load in q_loads:
+        load.wait()
 
 
 def pack(queries, keys_values, order):
@@ -79,21 +64,22 @@
         out_shape=jax.ShapeDtypeStruct((MB * KVH, rows, wide + 2 * HD), jnp.bfloat16),
         in_specs=[
             pl.BlockSpec(memory_space=pltpu.SMEM),
-            pl.BlockSpec(memory_space=pl.ANY),
-            pl.BlockSpec(memory_space=pl.ANY),
-        ],
-        out_specs=pl.BlockSpec(memory_space=pl.ANY),
+            pl.BlockSpec(memory_space=pltpu.HBM),
+            pl.BlockSpec(memory_space=pltpu.HBM),
+        ],
+        out_specs=pl.BlockSpec(memory_space=pltpu.VMEM),
         scratch_shapes=[
-            pltpu.VMEM((MB, KVH, rows, wide), jnp.bfloat16),
             pltpu.VMEM((MB, rows, KVH, 2 * HD), jnp.bfloat16),
-            pltpu.VMEM((MB, KVH, rows, 2 * HD), jnp.bfloat16),
             pltpu.SemaphoreType.DMA((MB, KVH)),
             pltpu.SemaphoreType.DMA((MB,)),
-            pltpu.SemaphoreType.DMA((MB, KVH)),
-            pltpu.SemaphoreType.DMA((MB, KVH)),
-        ],
+        ],
+        compiler_params=pltpu.CompilerParams(vmem_limit_bytes=12 << 20),
         name="pack",
-    )(order, queries, keys_values)
+    )(
+        order,
+        pltpu.with_memory_space_constraint(queries, pltpu.HBM),
+        pltpu.with_memory_space_constraint(keys_values, pltpu.HBM),
+    )
 
 
 def attend_kernel(
@@ -266,7 +252,8 @@
     packed = exchange(pack(queries, keys_values, order)).reshape(n_seq * rows, -1)
     near, far = attend(packed, lengths, order)
     far = handed_on(far)
-    near = handed_on(exchange(near.reshape(n_seq, rows, -1)))
+    near = exchange(near.reshape(n_seq, rows, -1))
+    near = handed_on(near)
     far = exchange(far.reshape(n_seq, rows, -1))
     return unpack(near, far)
 

time: 109 us -> 108 us (level)
  Pallas kernels: 18 us -> 16.9 us
    pallas_call x1, Pallas kernels: 4.78 us -> 3.05 us  [pack(): pl.pallas_call(pack_kernel, out_shape=jax.ShapeDtypeStruct((MB * KVH, row...]
where the time goes in v5:
time: 108 us; the launch traced here: 107 us
  blocking collectives  47.4 us (44%)
  waiting for transfers between devices  31.7 us (29%)
  Pallas kernels  16.9 us (16%)
  starting transfers between devices  10.8 us (10%)
    all_to_all x1, blocking collectives, exchange(): lax.all_to_all(blocks, 'seq', split_axis=0, concat_axis=0, tiled=True)  47.4 us
    all_to_all x2, waiting for transfers between devices, exchange(): lax.all_to_all(blocks, 'seq', split_axis=0, concat_axis=0, tiled=True)  23.4 us
    pallas_call x1, Pallas kernels, attend(): pl.pallas_call(attend_kernel, out_shape=[jax.ShapeDtypeStruct((tokens, ha...  12.2 us
    all_to_all x2, starting transfers between devices, exchange(): lax.all_to_all(blocks, 'seq', split_axis=0, concat_axis=0, tiled=True)  10.8 us
    ppermute x2, waiting for transfers between devices, handed_on(): lax.ppermute(block, 'section', [(i, (i + 1) % sections) for i in range(se...  8.28 us
    pallas_call x1, Pallas kernels, pack(): pl.pallas_call(pack_kernel, out_shape=jax.ShapeDtypeStruct((MB * KVH, row...  3.05 us
  transfers between devices with their start and end apart: 4, of which 4 were waited for; matrix products, arithmetic and copies ran while one was open for 0% of the time, Pallas kernels for 0%

profile of v5, /device:TPU:0, one launch (start us, length us, event | category | flops | bytes accessed | tf_op | source)
XLA Modules:
  0.0 107.5 jit_solution(9794609409408222464)
XLA Ops:
  0.0 0.0 copy-start
  0.0 0.7 copy-done
  0.7 3.0 %pack.1 = bf16[16,128,768]{2,1,0:T(8,128)(2,1)S(1)} custom-call(s32[1,2]{1,0:T(1,128)S(1)} %copy-done, bf16[1,2,128,4096]{3,2,1,0:T(8,128)(2,1)} %q_ref.1, bf16[1,2,128,8,256]{4,3,2,1,0:T(8,128)(2,1)} %kv_ref.1), custom_call_target="tpu_custom_call" | custom-call | tf_op jit(solution)/shard_map/pack/pallas_call | solution.py:62
  3.7 0.0 copy-start.1
  3.7 0.0 copy-start.2
  3.7 47.4 %all_to_all.15 = bf16[16,128,768]{2,1,0:T(8,128)(2,1)S(1)} all-to-all(bf16[16,128,768]{2,1,0:T(8,128)(2,1)S(1)} %pack.1), channel_id=1, replica_groups=mesh['section'=8,'seq'=16] {'seq'}, dimensions={0} | all-to-all | bytes 6291456 | tf_op jit(solution)/shard_map/all_to_all | solution.py:236
  51.1 0.0 copy-done.1
  51.2 0.0 copy-done.2
  51.2 12.2 %attend.1 = (bf16[2048,256]{1,0:T(8,128)(2,1)}, bf16[2048,256]{1,0:T(8,128)(2,1)S(1)}) custom-call(s32[1,2,4]{2,1,0:T(2,128)S(1)} %copy-done.2, s32[1,2]{1,0:T(1,128)S(1)} %copy-done.1, bf16[2048,768]{1,0:T(8,128)(2,1)S(1)} %bitcast.3), custom_call_target="tpu_custom_call" | custom-call | tf_op jit(solution)/shard_map/attend/pallas_call | solution.py:184
  63.4 3.7 %all-to-all-start.1 = ((bf16[16,128,256]{2,1,0:T(8,128)(2,1)}), bf16[16,128,256]{2,1,0:T(8,128)(2,1)S(1)}, u32[]{:S(2)}, u32[]{:S(2)}) async-start(bf16[16,128,256]{2,1,0:T(8,128)(2,1)} %bitcast.1), calls=%async_computation.1 | async-start | bytes 2097152 | tf_op jit(solution)/shard_map/all_to_all | solution.py:236
  67.1 0.0 collective-permute-start.1
  67.1 15.2 %all-to-all-done.1 = bf16[16,128,256]{2,1,0:T(8,128)(2,1)S(1)} async-done(((bf16[16,128,256]{2,1,0:T(8,128)(2,1)}), bf16[16,128,256]{2,1,0:T(8,128)(2,1)S(1)}, u32[]{:S(2)}, u32[]{:S(2)}) %all-to-all-start.1) | async-done | bytes 1048608 | tf_op jit(solution)/shard_map/all_to_all | solution.py:236
  82.3 0.0 collective-permute-start
  82.3 0.4 collective-permute-done.1
  82.6 7.1 %all-to-all-start.2 = ((bf16[16,128,256]{2,1,0:T(8,128)(2,1)}), bf16[16,128,256]{2,1,0:T(8,128)(2,1)S(1)}, u32[]{:S(2)}, u32[]{:S(2)}) async-start(bf16[16,128,256]{2,1,0:T(8,128)(2,1)} %bitcast.2), calls=%async_computation.2 | async-start | bytes 2097152 | tf_op jit(solution)/shard_map/all_to_all | solution.py:236
  89.8 7.9 %collective-permute-done.near_ref = bf16[16,128,256]{2,1,0:T(8,128)(2,1)S(1)} collective-permute-done((bf16[16,128,256]{2,1,0:T(8,128)(2,1)S(1)}, bf16[16,128,256]{2,1,0:T(8,128)(2,1)S(1)}, u32[]{:S(2)}, u32[]{:S(2)}) %collective-permute-start) | collective-permute-done | bytes 1048608 | tf_op jit(solution)/shard_map/ppermute | solution.py:246
  97.7 8.2 %all-to-all-done.2.far_ref = bf16[16,128,256]{2,1,0:T(8,128)(2,1)S(1)} async-done(((bf16[16,128,256]{2,1,0:T(8,128)(2,1)}), bf16[16,128,256]{2,1,0:T(8,128)(2,1)S(1)}, u32[]{:S(2)}, u32[]{:S(2)}) %all-to-all-start.2) | async-done | bytes 1048608 | tf_op jit(solution)/shard_map/all_to_all | solution.py:236
  105.9 1.6 %unpack.1 = bf16[1,2,128,4096]{3,2,1,0:T(8,128)(2,1)} custom-call(bf16[16,128,256]{2,1,0:T(8,128)(2,1)S(1)} %collective-permute-done.near_ref, bf16[16,128,256]{2,1,0:T(8,128)(2,1)S(1)} %all-to-all-done.2.far_ref), custom_call_target="tpu_custom_call" | custom-call | tf_op jit(solution)/shard_map/unpack/pallas_call | solution.py:224
Async XLA Ops:
  0.0 0.7 copy-start
  3.7 47.4 %copy-start.1 = (s32[1,2]{1,0:T(1,128)S(1)}, s32[1,2]{1,0:T(1,128)}, u32[]{:S(2)}) copy-start(s32[1,2]{1,0:T(1,128)} %order_ref.3) | copy-start | bytes 28
  3.7 47.4 %copy-start.2 = (s32[1,2,4]{2,1,0:T(2,128)S(1)}, s32[1,2,4]{2,1,0:T(2,128)}, u32[]{:S(2)}) copy-start(s32[1,2,4]{2,1,0:T(2,128)} %len_ref.1) | copy-start | bytes 100
  63.4 18.9 %all-to-all-start.1 = ((bf16[16,128,256]{2,1,0:T(8,128)(2,1)}), bf16[16,128,256]{2,1,0:T(8,128)(2,1)S(1)}, u32[]{:S(2)}, u32[]{:S(2)}) async-start(bf16[16,128,256]{2,1,0:T(8,128)(2,1)} %bitcast.1), calls=%async_computation.1 | async-start | bytes 2097152 | tf_op jit(solution)/shard_map/all_to_all | solution.py:236
  67.1 15.6 %collective-permute-start.1 = (bf16[2048,256]{1,0:T(8,128)(2,1)S(1)}, bf16[2048,256]{1,0:T(8,128)(2,1)}, u32[]{:S(2)}, u32[]{:S(2)}) collective-permute-start(bf16[2048,256]{1,0:T(8,128)(2,1)S(1)} %get-tuple-element.8), channel_id=1, source_target_pairs={{0,16},{16,32},{32,48},{48,64},{64,80},{80,96},{96,112},{112,0},{1... | collective-permute-start | bytes 3145736 | tf_op jit(solution)/shard_map/ppermute | solution.py:246
  82.3 15.4 %collective-permute-start = (bf16[16,128,256]{2,1,0:T(8,128)(2,1)S(1)}, bf16[16,128,256]{2,1,0:T(8,128)(2,1)S(1)}, u32[]{:S(2)}, u32[]{:S(2)}) collective-permute-start(bf16[16,128,256]{2,1,0:T(8,128)(2,1)S(1)} %all-to-all-done.1), channel_id=1, source_target_pairs={{0,16},{16,32},{32,48},{48,64},{64,80},{80,96},{96,112},{112,0},{1... | collective-permute-start | bytes 3145736 | tf_op jit(solution)/shard_map/ppermute | solution.py:246
  82.6 23.3 %all-to-all-start.2 = ((bf16[16,128,256]{2,1,0:T(8,128)(2,1)}), bf16[16,128,256]{2,1,0:T(8,128)(2,1)S(1)}, u32[]{:S(2)}, u32[]{:S(2)}) async-start(bf16[16,128,256]{2,1,0:T(8,128)(2,1)} %bitcast.2), calls=%async_computation.2 | async-start | bytes 2097152 | tf_op jit(solution)/shard_map/all_to_all | solution.py:236

commit v6 on v5

--- a/solution.py
+++ b/solution.py
@@ -145,12 +145,17 @@
 
             def mix(g):
                 peak = m_ref[g]
-                weights = [
-                    jnp.exp2(
-                        (s_ref[g, :, j * TILE : (j + 1) * TILE] - peak) * EXPONENT
-                    ).astype(jnp.bfloat16)
-                    for j in range(tiles)
-                ]
+
+                def weigh(rows, j):
+                    tile = s_ref[g, rows, j * TILE : (j + 1) * TILE]
+                    return jnp.exp2((tile - peak[rows]) * EXPONENT).astype(jnp.bfloat16)
+
+                weights = [weigh(slice(None), j) for j in range(tiles - 1)]
+                ends = []
+                for h in range(pair):
+                    ends.append(jnp.zeros((TILE, TILE), jnp.bfloat16))
+                    ends.append(weigh(slice(h * ROWS + TILE, (h + 1) * ROWS), tiles - 1))
+                weights.append(jnp.concatenate(ends, axis=0))
                 mixed = jnp.dot(
                     jnp.concatenate(weights, axis=1),
                     ve_ref[pl.ds(low, n * ROWS), :],

time: 108 us -> 108 us (level)
  no operation moved by 1% of the time
where the time goes in v6:
time: 108 us; the launch traced here: 107 us
  blocking collectives  47.4 us (44%)
  waiting for transfers between devices  31.7 us (29%)
  Pallas kernels  16.9 us (16%)
  starting transfers between devices  10.8 us (10%)
    all_to_all x1, blocking collectives, exchange(): lax.all_to_all(blocks, 'seq', split_axis=0, concat_axis=0, tiled=True)  47.4 us
    all_to_all x2, waiting for transfers between devices, exchange(): lax.all_to_all(blocks, 'seq', split_axis=0, concat_axis=0, tiled=True)  23.4 us
    pallas_call x1, Pallas kernels, attend(): pl.pallas_call(attend_kernel, out_shape=[jax.ShapeDtypeStruct((tokens, ha...  12.2 us
    all_to_all x2, starting transfers between devices, exchange(): lax.all_to_all(blocks, 'seq', split_axis=0, concat_axis=0, tiled=True)  10.8 us
    ppermute x2, waiting for transfers between devices, handed_on(): lax.ppermute(block, 'section', [(i, (i + 1) % sections) for i in range(se...  8.28 us
    pallas_call x1, Pallas kernels, pack(): pl.pallas_call(pack_kernel, out_shape=jax.ShapeDtypeStruct((MB * KVH, row...  3.05 us
  transfers between devices with their start and end apart: 4, of which 4 were waited for; matrix products, arithmetic and copies ran while one was open for 0% of the time, Pallas kernels for 0%

profile of v6, /device:TPU:0, one launch (start us, length us, event | category | flops | bytes accessed | tf_op | source)
XLA Modules:
  0.0 107.5 jit_solution(3796256239357073279)
XLA Ops:
  0.0 0.0 copy-start
  0.0 0.7 copy-done
  0.7 3.0 %pack.1 = bf16[16,128,768]{2,1,0:T(8,128)(2,1)S(1)} custom-call(s32[1,2]{1,0:T(1,128)S(1)} %copy-done, bf16[1,2,128,4096]{3,2,1,0:T(8,128)(2,1)} %q_ref.1, bf16[1,2,128,8,256]{4,3,2,1,0:T(8,128)(2,1)} %kv_ref.1), custom_call_target="tpu_custom_call" | custom-call | tf_op jit(solution)/shard_map/pack/pallas_call | solution.py:62
  3.7 0.0 copy-start.1
  3.7 0.0 copy-start.2
  3.7 47.4 %all_to_all.15 = bf16[16,128,768]{2,1,0:T(8,128)(2,1)S(1)} all-to-all(bf16[16,128,768]{2,1,0:T(8,128)(2,1)S(1)} %pack.1), channel_id=1, replica_groups=mesh['section'=8,'seq'=16] {'seq'}, dimensions={0} | all-to-all | bytes 6291456 | tf_op jit(solution)/shard_map/all_to_all | solution.py:241
  51.1 0.0 copy-done.1
  51.2 0.0 copy-done.2
  51.2 12.2 %attend.1 = (bf16[2048,256]{1,0:T(8,128)(2,1)}, bf16[2048,256]{1,0:T(8,128)(2,1)S(1)}) custom-call(s32[1,2,4]{2,1,0:T(2,128)S(1)} %copy-done.2, s32[1,2]{1,0:T(1,128)S(1)} %copy-done.1, bf16[2048,768]{1,0:T(8,128)(2,1)S(1)} %bitcast.3), custom_call_target="tpu_custom_call" | custom-call | tf_op jit(solution)/shard_map/attend/pallas_call | solution.py:189
  63.4 3.7 %all-to-all-start.1 = ((bf16[16,128,256]{2,1,0:T(8,128)(2,1)}), bf16[16,128,256]{2,1,0:T(8,128)(2,1)S(1)}, u32[]{:S(2)}, u32[]{:S(2)}) async-start(bf16[16,128,256]{2,1,0:T(8,128)(2,1)} %bitcast.1), calls=%async_computation.1 | async-start | bytes 2097152 | tf_op jit(solution)/shard_map/all_to_all | solution.py:241
  67.1 0.0 collective-permute-start.1
  67.1 15.2 %all-to-all-done.1 = bf16[16,128,256]{2,1,0:T(8,128)(2,1)S(1)} async-done(((bf16[16,128,256]{2,1,0:T(8,128)(2,1)}), bf16[16,128,256]{2,1,0:T(8,128)(2,1)S(1)}, u32[]{:S(2)}, u32[]{:S(2)}) %all-to-all-start.1) | async-done | bytes 1048608 | tf_op jit(solution)/shard_map/all_to_all | solution.py:241
  82.3 0.0 collective-permute-start
  82.3 0.4 collective-permute-done.1
  82.6 7.1 %all-to-all-start.2 = ((bf16[16,128,256]{2,1,0:T(8,128)(2,1)}), bf16[16,128,256]{2,1,0:T(8,128)(2,1)S(1)}, u32[]{:S(2)}, u32[]{:S(2)}) async-start(bf16[16,128,256]{2,1,0:T(8,128)(2,1)} %bitcast.2), calls=%async_computation.2 | async-start | bytes 2097152 | tf_op jit(solution)/shard_map/all_to_all | solution.py:241
  89.8 7.9 %collective-permute-done.near_ref = bf16[16,128,256]{2,1,0:T(8,128)(2,1)S(1)} collective-permute-done((bf16[16,128,256]{2,1,0:T(8,128)(2,1)S(1)}, bf16[16,128,256]{2,1,0:T(8,128)(2,1)S(1)}, u32[]{:S(2)}, u32[]{:S(2)}) %collective-permute-start) | collective-permute-done | bytes 1048608 | tf_op jit(solution)/shard_map/ppermute | solution.py:251
  97.7 8.2 %all-to-all-done.2.far_ref = bf16[16,128,256]{2,1,0:T(8,128)(2,1)S(1)} async-done(((bf16[16,128,256]{2,1,0:T(8,128)(2,1)}), bf16[16,128,256]{2,1,0:T(8,128)(2,1)S(1)}, u32[]{:S(2)}, u32[]{:S(2)}) %all-to-all-start.2) | async-done | bytes 1048608 | tf_op jit(solution)/shard_map/all_to_all | solution.py:241
  105.9 1.6 %unpack.1 = bf16[1,2,128,4096]{3,2,1,0:T(8,128)(2,1)} custom-call(bf16[16,128,256]{2,1,0:T(8,128)(2,1)S(1)} %collective-permute-done.near_ref, bf16[16,128,256]{2,1,0:T(8,128)(2,1)S(1)} %all-to-all-done.2.far_ref), custom_call_target="tpu_custom_call" | custom-call | tf_op jit(solution)/shard_map/unpack/pallas_call | solution.py:229
Async XLA Ops:
  0.0 0.7 copy-start
  3.7 47.4 %copy-start.1 = (s32[1,2]{1,0:T(1,128)S(1)}, s32[1,2]{1,0:T(1,128)}, u32[]{:S(2)}) copy-start(s32[1,2]{1,0:T(1,128)} %order_ref.3) | copy-start | bytes 28
  3.7 47.4 %copy-start.2 = (s32[1,2,4]{2,1,0:T(2,128)S(1)}, s32[1,2,4]{2,1,0:T(2,128)}, u32[]{:S(2)}) copy-start(s32[1,2,4]{2,1,0:T(2,128)} %len_ref.1) | copy-start | bytes 100
  63.4 18.9 %all-to-all-start.1 = ((bf16[16,128,256]{2,1,0:T(8,128)(2,1)}), bf16[16,128,256]{2,1,0:T(8,128)(2,1)S(1)}, u32[]{:S(2)}, u32[]{:S(2)}) async-start(bf16[16,128,256]{2,1,0:T(8,128)(2,1)} %bitcast.1), calls=%async_computation.1 | async-start | bytes 2097152 | tf_op jit(solution)/shard_map/all_to_all | solution.py:241
  67.1 15.6 %collective-permute-start.1 = (bf16[2048,256]{1,0:T(8,128)(2,1)S(1)}, bf16[2048,256]{1,0:T(8,128)(2,1)}, u32[]{:S(2)}, u32[]{:S(2)}) collective-permute-start(bf16[2048,256]{1,0:T(8,128)(2,1)S(1)} %get-tuple-element.8), channel_id=1, source_target_pairs={{0,16},{16,32},{32,48},{48,64},{64,80},{80,96},{96,112},{112,0},{1... | collective-permute-start | bytes 3145736 | tf_op jit(solution)/shard_map/ppermute | solution.py:251
  82.3 15.4 %collective-permute-start = (bf16[16,128,256]{2,1,0:T(8,128)(2,1)S(1)}, bf16[16,128,256]{2,1,0:T(8,128)(2,1)S(1)}, u32[]{:S(2)}, u32[]{:S(2)}) collective-permute-start(bf16[16,128,256]{2,1,0:T(8,128)(2,1)S(1)} %all-to-all-done.1), channel_id=1, source_target_pairs={{0,16},{16,32},{32,48},{48,64},{64,80},{80,96},{96,112},{112,0},{1... | collective-permute-start | bytes 3145736 | tf_op jit(solution)/shard_map/ppermute | solution.py:251
  82.6 23.3 %all-to-all-start.2 = ((bf16[16,128,256]{2,1,0:T(8,128)(2,1)}), bf16[16,128,256]{2,1,0:T(8,128)(2,1)S(1)}, u32[]{:S(2)}, u32[]{:S(2)}) async-start(bf16[16,128,256]{2,1,0:T(8,128)(2,1)} %bitcast.2), calls=%async_computation.2 | async-start | bytes 2097152 | tf_op jit(solution)/shard_map/all_to_all | solution.py:241
